TPU v7x, 512 devices: a whole 4x8x8 slice. The times are simulated.
512 devices in a mesh: leaf: 32 (over z, x), brick: 16 (over y, core).
Axes of the slice: x: 4, y: 8, z: 8, core: 2. Of those that a mesh axis runs over, the one named last changes fastest.
Arguments:
- points: bfloat16 [64, 32, 2, 3, 256], P('leaf', 'brick'), may hold values from 0 to 1
- test_matrix: bfloat16 [64, 32, 2, 64, 256], P('leaf', 'brick'), may hold values from -40 to 40
- trunc_ranks: int32 [5], replicated, may hold values from 32 to 64, as said below
Outputs:
- leaf_basis: bfloat16 [64, 32, 2, 64, 256], P('leaf', 'brick')
- leaf_transfer: float32 [64, 32, 2, 64, 64], P('leaf', 'brick')
- upper_transfer: float32 [3, 32, 16, 64, 64], P(None, 'leaf', 'brick')
- top_sample: float32 [32, 16, 64, 64], P('leaf', 'brick')
Inputs may be any that keep to these rules, and one draw needn't show every extreme that they name: `trunc_ranks`: one level keeps 64 rows and another keeps 64 // 2.
All inputs are finite; a program needn't handle non-finite values.
Results may differ from a plain program's by a relative error of at most 0.0085.
The roundings to bfloat16 on the way count: a program that leaves them out, or rounds other values in their place, can miss the bound.
Values may be sent and summed in bfloat16 or wider, within the bound.
No kernel may reach another device: no remote copies, remote signals or barrier semaphores. Data moves between devices by JAX's collectives and lax.ppermute only.
A program may use at most 64 MiB of HBM per device.

v0:
```python
import math

import jax
import jax.numpy as jnp
from jax import lax
from jax.sharding import PartitionSpec as P

LEVELS = 4


ROOT_THREE = math.sqrt(3.0)
SHIFT_SHARE = 0.01
TINY = 1e-06
HIGH = lax.Precision.HIGHEST
NEIGHBOUR_OFFSETS = [
    (off_x, off_y, off_z) for off_x in (-1, 0, 1) for off_y in (-1, 0, 1) for off_z in (-1, 0, 1)
]


def with_halo(cells, sides, width):
    for axis, dim in sides:
        count = lax.axis_size(axis)
        ends = count - 1
        head = lax.slice_in_dim(cells, 0, width, axis=dim)
        tail = lax.slice_in_dim(cells, cells.shape[dim] - width, cells.shape[dim], axis=dim)
        cells = jnp.concatenate(
            [
                lax.ppermute(tail, axis, [(i, (i + 1) % count) for i in range(ends)]),
                cells,
                lax.ppermute(head, axis, [((i + 1) % count, i) for i in range(ends)]),
            ],
            axis=dim,
        )
    return cells


def swapped(value, axis, stride):
    return lax.ppermute(value, axis, [(i, i ^ 1 << stride) for i in range(lax.axis_size(axis))])


def matern(near_points, own_points, offset):
    summed = 0.0
    for axis_id in range(3):
        spacing = (
            offset[axis_id] + near_points[..., axis_id, :, None] - own_points[..., axis_id, None, :]
        )
        summed = summed + spacing * spacing
    scaled = ROOT_THREE * jnp.sqrt(summed)
    return (1.0 + scaled) * jnp.exp(-scaled)


def factor(gram_sum):
    trace_sum = jnp.trace(gram_sum, axis1=-2, axis2=-1)
    shift_term = SHIFT_SHARE * trace_sum / gram_sum.shape[-1] + TINY
    identity = jnp.eye(gram_sum.shape[-1], dtype=gram_sum.dtype)
    factor_low = jnp.linalg.cholesky(gram_sum + shift_term[..., None, None] * identity)
    return (factor_low, trace_sum)


def solve_low(factor_low, right_side):
    return jax.scipy.linalg.solve_triangular(factor_low, right_side, lower=True)


def keep_rows(trunc_ranks, height, sample_width):
    return (jnp.arange(sample_width, dtype=jnp.int32) < trunc_ranks[height]).astype(jnp.float32)[
        :, None
    ]


def leaf_level(sample, keep):
    gram_sum = jnp.einsum("...sp,...tp->...st", sample, sample, precision=HIGH)
    factor_low, trace_sum = factor(gram_sum)
    basis_rows = solve_low(factor_low, sample) * keep
    projected = solve_low(factor_low, gram_sum) * keep
    return (basis_rows, projected)


def merge_level(projected, keep):
    grid_x, grid_y, grid_z = (projected.shape[0], projected.shape[1], projected.shape[2])
    sample_width = projected.shape[-1]
    fold_x = 2
    fold_y = 2
    fold_z = 2
    children = projected.reshape(
        grid_x // fold_x,
        fold_x,
        grid_y // fold_y,
        fold_y,
        grid_z // fold_z,
        fold_z,
        sample_width,
        sample_width,
    )
    gram_sum = jnp.einsum("aibjcksu,aibjcksv->abcuv", children, children, precision=HIGH)
    factor_low, trace_sum = factor(gram_sum)
    spread = jnp.broadcast_to(factor_low[:, None, :, None, :, None], children.shape)
    transfer = solve_low(spread, jnp.swapaxes(children, -1, -2)) * keep
    transfer = transfer.reshape(projected.shape)
    parent = solve_low(factor_low, gram_sum) * keep
    return (transfer, parent, trace_sum)


def shards(points, test_matrix, trunc_ranks):
    near_points, near_tests = (
        with_halo(points, (("leaf", 0), ("brick", 1)), 1),
        with_halo(test_matrix, (("leaf", 0), ("brick", 1)), 1),
    )
    widths = ((0, 0), (0, 0), (1, 1), (0, 0), (0, 0))
    near_points = jnp.pad(near_points, widths).astype(jnp.float32)
    near_tests = jnp.pad(near_tests, widths)
    own_points = points.astype(jnp.float32)
    block_x, block_y, block_z = (points.shape[0], points.shape[1], points.shape[2])
    sample_width = test_matrix.shape[3]
    scale_up = math.sqrt(sample_width)
    running = jnp.zeros((block_x, block_y, block_z, sample_width, points.shape[4]), jnp.float32)
    for off_x, off_y, off_z in NEIGHBOUR_OFFSETS:
        neighbour_points = near_points[
            1 + off_x : 1 + off_x + block_x,
            1 + off_y : 1 + off_y + block_y,
            1 + off_z : 1 + off_z + block_z,
        ]
        neighbour_tests = near_tests[
            1 + off_x : 1 + off_x + block_x,
            1 + off_y : 1 + off_y + block_y,
            1 + off_z : 1 + off_z + block_z,
        ]
        kernel_tile = matern(
            neighbour_points, own_points, (float(off_x), float(off_y), float(off_z))
        ).astype(jnp.bfloat16)
        running = running + jnp.einsum(
            "xyzsq,xyzqp->xyzsp", neighbour_tests, kernel_tile, preferred_element_type=jnp.float32
        )
    basis_rows, projected = leaf_level(running, keep_rows(trunc_ranks, 0, sample_width))
    leaf_basis = (basis_rows * math.sqrt(points.shape[-1])).astype(jnp.bfloat16)
    transfer, projected, trace_sum = merge_level(projected, keep_rows(trunc_ranks, 1, sample_width))
    leaf_transfer = transfer * scale_up
    uppers = []
    current = projected[0, 0, 0]
    for height in range(2, LEVELS + 1):
        bit_place = height - 2
        gram_sum = jnp.dot(current.T, current, precision=HIGH, preferred_element_type=jnp.float32)
        gram_sum = gram_sum + swapped(gram_sum, "leaf", bit_place)
        gram_sum = gram_sum + swapped(gram_sum, "brick", bit_place)
        keep = keep_rows(trunc_ranks, height, sample_width)
        factor_low, trace_sum = factor(gram_sum)
        uppers.append(solve_low(factor_low, current.T) * keep * scale_up)
        current = solve_low(factor_low, gram_sum) * keep
    top_sample = current / jnp.sqrt(trace_sum / sample_width + TINY)
    upper_transfer = jnp.stack(uppers)[:, None, None]
    return (leaf_basis, leaf_transfer, upper_transfer, top_sample[None, None])


def solution(mesh):
    placed = (P("leaf", "brick", None, None, None), P("leaf", "brick", None, None, None), P())
    return jax.shard_map(
        shards,
        mesh=mesh,
        in_specs=placed,
        out_specs=(
            P("leaf", "brick", None, None, None),
            P("leaf", "brick", None, None, None),
            P(None, "leaf", "brick", None, None),
            P("leaf", "brick", None, None),
        ),
        check_vma=False,
    )
```

profile of v0, /device:TPU:152, one launch (start us, length us, event | category | flops | bytes accessed | tf_op | source)
XLA Modules:
  0.0 311.1 jit_solution(8985794354781397508)
XLA Ops:
  1.6 3.4 %collective-permute-start = (bf16[1,2,2,64,256]{4,3,2,1,0:T(8,128)(2,1)S(1)}, bf16[1,2,2,64,256]{4,3,2,1,0:T(8,128)(2,1)S(1)}, u32[]{:S(2)}, u32[]{:S(2)}) collective-permute-start(bf16[1,2,2,64,256]{4,3,2,1,0:T(8,128)(2,1)S(1)} %get-tuple-element.26), channel_id=1, source_target_pairs={{0,16},{16,32},{32,48},{48,64},{64,80},{80,96},{96,112},{112,128},... | collective-permute-start | bytes 393224 | tf_op jit(solution)/shard_map/ppermute | solution.py:28
  5.1 4.6 %collective-permute-start.1 = (bf16[1,2,2,64,256]{4,3,2,1,0:T(8,128)(2,1)S(1)}, bf16[1,2,2,64,256]{4,3,2,1,0:T(8,128)(2,1)S(1)}, u32[]{:S(2)}, u32[]{:S(2)}) collective-permute-start(bf16[1,2,2,64,256]{4,3,2,1,0:T(8,128)(2,1)S(1)} %get-tuple-element.25), channel_id=1, source_target_pairs={{16,0},{32,16},{48,32},{64,48},{80,64},{96,80},{112,96},{128,112},... | collective-permute-start | bytes 393224 | tf_op jit(solution)/shard_map/ppermute | solution.py:30
  11.6 6.0 %collective-permute-start.5 = (bf16[1,2,2,3,256]{4,2,3,1,0:T(2,128)(2,1)S(1)}, bf16[1,2,2,3,256]{4,2,3,1,0:T(2,128)(2,1)S(1)}, u32[]{:S(2)}, u32[]{:S(2)}) collective-permute-start(bf16[1,2,2,3,256]{4,2,3,1,0:T(2,128)(2,1)S(1)} %get-tuple-element.115), channel_id=1, source_target_pairs={{16,0},{32,16},{48,32},{64,48},{80,64},{96,80},{112,96},{128,112},... | collective-permute-start | bytes 18440 | tf_op jit(solution)/shard_map/ppermute | solution.py:30
  23.2 3.6 %collective-permute-start.7 = (bf16[4,1,2,3,256]{4,2,3,1,0:T(2,128)(2,1)S(1)}, bf16[4,1,2,3,256]{4,2,3,1,0:T(2,128)(2,1)S(1)}, u32[]{:S(2)}, u32[]{:S(2)}) collective-permute-start(bf16[4,1,2,3,256]{4,2,3,1,0:T(2,128)(2,1)S(1)} %get-tuple-element.112), channel_id=1, source_target_pairs={{1,0},{2,1},{3,2},{4,3},{5,4},{6,5},{7,6},{8,7},{9,8},{10,9},{11,1... | collective-permute-start | bytes 36872 | tf_op jit(solution)/shard_map/ppermute | solution.py:30
  29.8 2.3 convolution_bitcast_fusion
  32.3 5.6 %collective-permute-start.2 = (bf16[4,1,2,64,256]{4,3,2,1,0:T(8,128)(2,1)S(1)}, bf16[4,1,2,64,256]{4,3,2,1,0:T(8,128)(2,1)S(1)}, u32[]{:S(2)}, u32[]{:S(2)}) collective-permute-start(bf16[4,1,2,64,256]{4,3,2,1,0:T(8,128)(2,1)S(1)} %get-tuple-element.23), channel_id=1, source_target_pairs={{0,1},{1,2},{2,3},{3,4},{4,5},{5,6},{6,7},{7,8},{8,9},{9,10},{10,1... | collective-permute-start | bytes 786440 | tf_op jit(solution)/shard_map/ppermute | solution.py:28
  39.8 2.3 fusion.59
  42.2 2.9 fusion.60
  74.0 1.9 fusion.54
  75.9 1.9 fusion.55
  77.8 1.9 fusion.56
  79.8 1.9 fusion.57
  83.6 2.3 fusion.53
  86.0 2.2 fusion.25
  89.1 46.9 %custom-call.20 = f32[2,2,2,64,64]{4,3,2,1,0:T(8,128)S(1)} custom-call(f32[2,2,2,64,64]{4,3,2,1,0:T(8,128)S(1)} %fusion.288), custom_call_target="Cholesky" | custom-call | tf_op jit(solution)/shard_map/jit(cholesky)/cholesky | solution.py:56
  136.3 39.3 %custom-call.21 = f32[2,2,2,1,64,64]{4,5,3,2,1,0:T(8,128)S(1)} custom-call(f32[2,2,2,1,64,64]{5,4,3,2,1,0:T(8,128)S(1)} %select_bitcast_fusion.1), custom_call_target="InvertDiagBlocksLowerTriangular" | custom-call | tf_op jit(solution)/shard_map/jit(_solve_triangular)/vmap(vmap(vmap()))/triangular_solve | solution.py:61
  178.4 5.9 %custom-call.22 = f32[1,1,1,64,64]{4,3,2,1,0:T(8,128)S(1)} custom-call(f32[1,1,1,64,64]{4,3,2,1,0:T(8,128)S(1)} %copy.40), custom_call_target="Cholesky" | custom-call | tf_op jit(solution)/shard_map/jit(cholesky)/cholesky | solution.py:56
  185.6 4.9 %custom-call.32 = f32[1,64,64]{1,2,0:T(8,128)S(1)} custom-call(f32[1,64,64]{2,1,0:T(8,128)S(1)} %get-tuple-element.21), custom_call_target="InvertDiagBlocksLowerTriangular" | custom-call | tf_op jit(solution)/shard_map/jit(_solve_triangular)/triangular_solve/custom-call.5 | solution.py:61
  193.6 3.2 %collective-permute-done.8 = f32[64,64]{0,1:T(8,128)S(1)} collective-permute-done((f32[64,64]{0,1:T(8,128)S(1)}, f32[64,64]{0,1:T(8,128)S(1)}, u32[]{:S(2)}, u32[]{:S(2)}) %collective-permute-start.8) | collective-permute-done | bytes 16416 | tf_op jit(solution)/shard_map/ppermute | solution.py:38
  196.8 2.5 collective-permute-start.9
  202.1 5.8 %cholesky.144 = f32[64,64]{1,0:T(8,128)S(1)} custom-call(f32[64,64]{1,0:T(8,128)S(1)} %fusion.305), custom_call_target="Cholesky" | custom-call | tf_op jit(solution)/shard_map/jit(cholesky)/cholesky | solution.py:56
  209.3 4.9 %custom-call.33 = f32[1,64,64]{1,2,0:T(8,128)S(1)} custom-call(f32[1,64,64]{2,1,0:T(8,128)S(1)} %fusion.291), custom_call_target="InvertDiagBlocksLowerTriangular" | custom-call | tf_op jit(solution)/shard_map/jit(_solve_triangular)/triangular_solve/custom-call.5 | solution.py:61
  214.7 4.6 %collective-permute-start.10 = (f32[64,64]{0,1:T(8,128)S(1)}, f32[64,64]{0,1:T(8,128)S(1)}, u32[]{:S(2)}, u32[]{:S(2)}) collective-permute-start(f32[64,64]{0,1:T(8,128)S(1)} %fusion.433), channel_id=1, source_target_pairs={{0,32},{16,48},{32,0},{48,16},{64,96},{80,112},{96,64},{112,80},{1... | collective-permute-start | bytes 49160 | tf_op jit(solution)/shard_map/ppermute | solution.py:38
  219.3 39.3 %custom-call.31 = f32[2,2,2,1,64,64]{4,5,3,2,1,0:T(8,128)S(1)} custom-call(f32[2,2,2,1,64,64]{5,4,3,2,1,0:T(8,128)S(1)} %select_bitcast_fusion), custom_call_target="InvertDiagBlocksLowerTriangular" | custom-call | tf_op jit(solution)/shard_map/jit(_solve_triangular)/vmap(vmap(vmap()))/triangular_solve/custom-call.4 | solution.py:61
  258.7 2.1 collective-permute-start.11
  262.1 2.4 collective-permute-done.11
  265.9 5.8 %cholesky.155 = f32[64,64]{1,0:T(8,128)S(1)} custom-call(f32[64,64]{1,0:T(8,128)S(1)} %fusion.301), custom_call_target="Cholesky" | custom-call | tf_op jit(solution)/shard_map/jit(cholesky)/cholesky | solution.py:56
  273.1 4.9 %custom-call.35 = f32[1,64,64]{1,2,0:T(8,128)S(1)} custom-call(f32[1,64,64]{2,1,0:T(8,128)S(1)} %fusion.292), custom_call_target="InvertDiagBlocksLowerTriangular" | custom-call | tf_op jit(solution)/shard_map/jit(_solve_triangular)/triangular_solve/custom-call.5 | solution.py:61
  278.5 7.9 %collective-permute-start.12 = (f32[64,64]{0,1:T(8,128)S(1)}, f32[64,64]{0,1:T(8,128)S(1)}, u32[]{:S(2)}, u32[]{:S(2)}) collective-permute-start(f32[64,64]{0,1:T(8,128)S(1)} %fusion.434), channel_id=1, source_target_pairs={{0,64},{16,80},{32,96},{48,112},{64,0},{80,16},{96,32},{112,48},{1... | collective-permute-start | bytes 49160 | tf_op jit(solution)/shard_map/ppermute | solution.py:38
  290.4 4.5 %collective-permute-done.13 = f32[64,64]{0,1:T(8,128)S(1)} collective-permute-done((f32[64,64]{0,1:T(8,128)S(1)}, f32[64,64]{0,1:T(8,128)S(1)}, u32[]{:S(2)}, u32[]{:S(2)}) %collective-permute-start.13) | collective-permute-done | bytes 16416 | tf_op jit(solution)/shard_map/ppermute | solution.py:38
  296.3 5.8 %cholesky.166 = f32[64,64]{1,0:T(8,128)S(1)} custom-call(f32[64,64]{1,0:T(8,128)S(1)} %fusion.297), custom_call_target="Cholesky" | custom-call | tf_op jit(solution)/shard_map/jit(cholesky)/cholesky | solution.py:56
  303.5 4.9 %custom-call.37 = f32[1,64,64]{1,2,0:T(8,128)S(1)} custom-call(f32[1,64,64]{2,1,0:T(8,128)S(1)} %fusion.293), custom_call_target="InvertDiagBlocksLowerTriangular" | custom-call | tf_op jit(solution)/shard_map/jit(_solve_triangular)/triangular_solve/custom-call.5 | solution.py:61
  (125 shorter events, 67.3 us)
Async XLA Ops:
  0.6 9.0 %copy-start.1 = (bf16[2,2,2,3,256]{4,2,3,1,0:T(2,128)(2,1)S(1)}, bf16[2,2,2,3,256]{4,2,3,1,0:T(2,128)(2,1)}, u32[]{:S(2)}) copy-start(bf16[2,2,2,3,256]{4,2,3,1,0:T(2,128)(2,1)} %param.8) | copy-start | bytes 36868
  0.6 17.0 %copy-start.2 = (s32[5]{0:T(128)S(1)}, s32[5]{0:T(128)}, u32[]{:S(2)}) copy-start(s32[5]{0:T(128)} %param.10) | copy-start | bytes 64
  1.6 30.5 %collective-permute-start = (bf16[1,2,2,64,256]{4,3,2,1,0:T(8,128)(2,1)S(1)}, bf16[1,2,2,64,256]{4,3,2,1,0:T(8,128)(2,1)S(1)}, u32[]{:S(2)}, u32[]{:S(2)}) collective-permute-start(bf16[1,2,2,64,256]{4,3,2,1,0:T(8,128)(2,1)S(1)} %get-tuple-element.26), channel_id=1, source_target_pairs={{0,16},{16,32},{32,48},{48,64},{64,80},{80,96},{96,112},{112,128},... | collective-permute-start | bytes 393224 | tf_op jit(solution)/shard_map/ppermute | solution.py:28
  5.1 27.2 %collective-permute-start.1 = (bf16[1,2,2,64,256]{4,3,2,1,0:T(8,128)(2,1)S(1)}, bf16[1,2,2,64,256]{4,3,2,1,0:T(8,128)(2,1)S(1)}, u32[]{:S(2)}, u32[]{:S(2)}) collective-permute-start(bf16[1,2,2,64,256]{4,3,2,1,0:T(8,128)(2,1)S(1)} %get-tuple-element.25), channel_id=1, source_target_pairs={{16,0},{32,16},{48,32},{64,48},{80,64},{96,80},{112,96},{128,112},... | collective-permute-start | bytes 393224 | tf_op jit(solution)/shard_map/ppermute | solution.py:30
  9.6 11.6 %collective-permute-start.4 = (bf16[1,2,2,3,256]{4,2,3,1,0:T(2,128)(2,1)S(1)}, bf16[1,2,2,3,256]{4,2,3,1,0:T(2,128)(2,1)S(1)}, u32[]{:S(2)}, u32[]{:S(2)}) collective-permute-start(bf16[1,2,2,3,256]{4,2,3,1,0:T(2,128)(2,1)S(1)} %get-tuple-element.116), channel_id=1, source_target_pairs={{0,16},{16,32},{32,48},{48,64},{64,80},{80,96},{96,112},{112,128},... | collective-permute-start | bytes 18440 | tf_op jit(solution)/shard_map/ppermute | solution.py:28
  11.6 9.7 %collective-permute-start.5 = (bf16[1,2,2,3,256]{4,2,3,1,0:T(2,128)(2,1)S(1)}, bf16[1,2,2,3,256]{4,2,3,1,0:T(2,128)(2,1)S(1)}, u32[]{:S(2)}, u32[]{:S(2)}) collective-permute-start(bf16[1,2,2,3,256]{4,2,3,1,0:T(2,128)(2,1)S(1)} %get-tuple-element.115), channel_id=1, source_target_pairs={{16,0},{32,16},{48,32},{64,48},{80,64},{96,80},{112,96},{128,112},... | collective-permute-start | bytes 18440 | tf_op jit(solution)/shard_map/ppermute | solution.py:30
  21.3 5.6 %collective-permute-start.6 = (bf16[4,1,2,3,256]{4,2,3,1,0:T(2,128)(2,1)S(1)}, bf16[4,1,2,3,256]{4,2,3,1,0:T(2,128)(2,1)S(1)}, u32[]{:S(2)}, u32[]{:S(2)}) collective-permute-start(bf16[4,1,2,3,256]{4,2,3,1,0:T(2,128)(2,1)S(1)} %get-tuple-element.111), channel_id=1, source_target_pairs={{0,1},{1,2},{2,3},{3,4},{4,5},{5,6},{6,7},{7,8},{8,9},{9,10},{10,1... | collective-permute-start | bytes 36872 | tf_op jit(solution)/shard_map/ppermute | solution.py:28
  23.2 5.5 %collective-permute-start.7 = (bf16[4,1,2,3,256]{4,2,3,1,0:T(2,128)(2,1)S(1)}, bf16[4,1,2,3,256]{4,2,3,1,0:T(2,128)(2,1)S(1)}, u32[]{:S(2)}, u32[]{:S(2)}) collective-permute-start(bf16[4,1,2,3,256]{4,2,3,1,0:T(2,128)(2,1)S(1)} %get-tuple-element.112), channel_id=1, source_target_pairs={{1,0},{2,1},{3,2},{4,3},{5,4},{6,5},{7,6},{8,7},{9,8},{10,9},{11,1... | collective-permute-start | bytes 36872 | tf_op jit(solution)/shard_map/ppermute | solution.py:30
  28.9 1.0 copy-start
  32.3 12.7 %collective-permute-start.2 = (bf16[4,1,2,64,256]{4,3,2,1,0:T(8,128)(2,1)S(1)}, bf16[4,1,2,64,256]{4,3,2,1,0:T(8,128)(2,1)S(1)}, u32[]{:S(2)}, u32[]{:S(2)}) collective-permute-start(bf16[4,1,2,64,256]{4,3,2,1,0:T(8,128)(2,1)S(1)} %get-tuple-element.23), channel_id=1, source_target_pairs={{0,1},{1,2},{2,3},{3,4},{4,5},{5,6},{6,7},{7,8},{8,9},{9,10},{10,1... | collective-permute-start | bytes 786440 | tf_op jit(solution)/shard_map/ppermute | solution.py:28
  37.9 7.2 %collective-permute-start.3 = (bf16[4,1,2,64,256]{4,3,2,1,0:T(8,128)(2,1)S(1)}, bf16[4,1,2,64,256]{4,3,2,1,0:T(8,128)(2,1)S(1)}, u32[]{:S(2)}, u32[]{:S(2)}) collective-permute-start(bf16[4,1,2,64,256]{4,3,2,1,0:T(8,128)(2,1)S(1)} %get-tuple-element.24), channel_id=1, source_target_pairs={{1,0},{2,1},{3,2},{4,3},{5,4},{6,5},{7,6},{8,7},{9,8},{10,9},{11,1... | collective-permute-start | bytes 786440 | tf_op jit(solution)/shard_map/ppermute | solution.py:30
  191.0 5.8 %collective-permute-start.8 = (f32[64,64]{0,1:T(8,128)S(1)}, f32[64,64]{0,1:T(8,128)S(1)}, u32[]{:S(2)}, u32[]{:S(2)}) collective-permute-start(f32[64,64]{0,1:T(8,128)S(1)} %fusion.432), channel_id=1, source_target_pairs={{0,16},{16,0},{32,48},{48,32},{64,80},{80,64},{96,112},{112,96},{1... | collective-permute-start | bytes 49160 | tf_op jit(solution)/shard_map/ppermute | solution.py:38
  196.8 3.9 %collective-permute-start.9 = (f32[64,64]{0,1:T(8,128)S(1)}, f32[64,64]{0,1:T(8,128)S(1)}, u32[]{:S(2)}, u32[]{:S(2)}) collective-permute-start(f32[64,64]{0,1:T(8,128)S(1)} %add.1234), channel_id=1, source_target_pairs={{0,1},{1,0},{2,3},{3,2},{4,5},{5,4},{6,7},{7,6},{8,9},{9,8},{10,11... | collective-permute-start | bytes 49160 | tf_op jit(solution)/shard_map/ppermute | solution.py:38
  214.7 44.0 %collective-permute-start.10 = (f32[64,64]{0,1:T(8,128)S(1)}, f32[64,64]{0,1:T(8,128)S(1)}, u32[]{:S(2)}, u32[]{:S(2)}) collective-permute-start(f32[64,64]{0,1:T(8,128)S(1)} %fusion.433), channel_id=1, source_target_pairs={{0,32},{16,48},{32,0},{48,16},{64,96},{80,112},{96,64},{112,80},{1... | collective-permute-start | bytes 49160 | tf_op jit(solution)/shard_map/ppermute | solution.py:38
  258.7 5.8 %collective-permute-start.11 = (f32[64,64]{0,1:T(8,128)S(1)}, f32[64,64]{0,1:T(8,128)S(1)}, u32[]{:S(2)}, u32[]{:S(2)}) collective-permute-start(f32[64,64]{0,1:T(8,128)S(1)} %add.1238), channel_id=1, source_target_pairs={{0,2},{1,3},{2,0},{3,1},{4,6},{5,7},{6,4},{7,5},{8,10},{9,11},{10,... | collective-permute-start | bytes 49160 | tf_op jit(solution)/shard_map/ppermute | solution.py:38
  278.5 9.8 %collective-permute-start.12 = (f32[64,64]{0,1:T(8,128)S(1)}, f32[64,64]{0,1:T(8,128)S(1)}, u32[]{:S(2)}, u32[]{:S(2)}) collective-permute-start(f32[64,64]{0,1:T(8,128)S(1)} %fusion.434), channel_id=1, source_target_pairs={{0,64},{16,80},{32,96},{48,112},{64,0},{80,16},{96,32},{112,48},{1... | collective-permute-start | bytes 49160 | tf_op jit(solution)/shard_map/ppermute | solution.py:38
  288.3 6.7 %collective-permute-start.13 = (f32[64,64]{0,1:T(8,128)S(1)}, f32[64,64]{0,1:T(8,128)S(1)}, u32[]{:S(2)}, u32[]{:S(2)}) collective-permute-start(f32[64,64]{0,1:T(8,128)S(1)} %add.1242), channel_id=1, source_target_pairs={{0,4},{1,5},{2,6},{3,7},{4,0},{5,1},{6,2},{7,3},{8,12},{9,13},{10,... | collective-permute-start | bytes 49160 | tf_op jit(solution)/shard_map/ppermute | solution.py:38
where the time goes:
time: 314 us; the launch traced here: 311 us
  other arithmetic  181 us (58%)
  matrix products  58 us (18%)
  starting transfers between devices  49.9 us (16%)
  waiting for transfers between devices  13.6 us (4%)
  between operations  5.01 us (2%)
  local copies, waits for them, and re-layouts  3.31 us (1%)
    another operation x13, other arithmetic, solve_low(): return jax.scipy.linalg.solve_triangular(factor_low, right_side, lower=True)  101 us
    another operation x16, other arithmetic, factor(): jnp.linalg.cholesky(gram_sum + shift_term[..., None, None] * identity)  73.2 us
    dot_general x27, matrix products, shards(): jnp.einsum('xyzsq,xyzqp->xyzsp', neighbour_tests, kernel_tile, preferred_...  50.4 us
    ppermute x6, starting transfers between devices, swapped(): lax.ppermute(value, axis, [(i, i ^ 1 << stride) for i in range(lax.axis_s...  20.9 us
    ppermute x4, starting transfers between devices, with_halo(): lax.ppermute(head, axis, [((i + 1) % count, i) for i in range(ends)])  16.1 us
    ppermute x4, starting transfers between devices, with_halo(): lax.ppermute(tail, axis, [(i, (i + 1) % count) for i in range(ends)])  12.8 us
    ppermute x6, waiting for transfers between devices, swapped(): lax.ppermute(value, axis, [(i, i ^ 1 << stride) for i in range(lax.axis_s...  11.8 us
  transfers between devices with their start and end apart: 14, of which 5 were waited for; matrix products, arithmetic and copies ran while one was open for 18% of the time, Pallas kernels for 0%

commit v1 on v0

v1 whole, which is shorter than its diff:
```python
import functools
import math

import jax
import jax.numpy as jnp
from jax import lax
from jax.experimental import pallas as pl
from jax.experimental.pallas import tpu as pltpu
from jax.sharding import PartitionSpec as P

LEVELS = 4
EXP_SCALE = -1.0 / math.log(2.0)
AHEAD = 1
BEHIND = 1
SHIFT_SHARE = 0.01
TINY = 1e-06
HIGH = lax.Precision.HIGHEST
F32 = jnp.float32
BF16 = jnp.bfloat16
S = 64
N = 256
FEAT = 32
LEAF_PAIRS = 4
LEAF_PANEL = 4
ONE_PANEL = 8


def split_square(x):
    sq = x * x
    hi = sq.astype(BF16).astype(F32)
    return hi, sq - hi


def left_rows(pts):
    x = pts.astype(F32)
    hi, lo = split_square(x)
    threes = jnp.full((10, N), 3.0, F32)
    zeros = jnp.zeros((FEAT - 25, N), F32)
    return jnp.concatenate([-2.0 * x, -2.0 * x, hi, lo, x, threes, zeros], axis=0)


def right_rows(pts):
    x = pts.astype(F32)
    hi, lo = split_square(x)
    tripled = 3.0 * x
    coarse = tripled.astype(BF16).astype(F32)
    zero3 = jnp.zeros((3, N), F32)
    three3 = jnp.full((3, N), 3.0, F32)
    tail = jnp.zeros((FEAT - 25, N), F32)
    base = jnp.concatenate(
        [coarse, tripled - coarse, three3, three3, zero3, hi, lo, zero3, zero3[:1], tail], axis=0
    )
    slope = jnp.concatenate(
        [zero3] * 4 + [2.0 * three3, zero3, zero3, -2.0 * x, zero3[:1] + 1.0, tail], axis=0
    )
    return base, slope


def put_left(pts, left_ref, slot):
    left_ref[slot] = left_rows(pts).T.astype(BF16)


def put_right(pts, base_ref, slope_ref, slot):
    base, slope = right_rows(pts)
    base_ref[slot] = base
    slope_ref[slot] = slope


def offset_rows(off):
    row = lax.broadcasted_iota(jnp.int32, (FEAT, N), 0)
    ox, oy, oz = (jnp.asarray(o, F32) for o in off)
    total = ox * ox + oy * oy + oz * oz
    out = jnp.where((row == 12) | (row == 21), ox, total)
    out = jnp.where((row == 13) | (row == 22), oy, out)
    return jnp.where((row == 14) | (row == 23), oz, out)


def square_tile(left, base, slope, off):
    right = (base + offset_rows(off) * slope).astype(BF16)
    return jnp.dot(left, right, preferred_element_type=F32)


def matern(sq):
    sq = jnp.maximum(sq, 1e-30)
    scaled = sq * lax.rsqrt(sq)
    return ((1.0 + scaled) * jnp.exp2(scaled * EXP_SCALE)).astype(BF16)


def pipelined(squares, uses):
    ahead = [squares[k]() for k in range(min(AHEAD, len(squares)))]
    waiting = []
    for k in range(len(squares)):
        if k + AHEAD < len(squares):
            ahead.append(squares[k + AHEAD]())
        waiting.append((uses[k], matern(ahead.pop(0))))
        if len(waiting) > BEHIND:
            use, tile = waiting.pop(0)
            use(tile)
    for use, tile in waiting:
        use(tile)


def bits(box):
    return box >> 2, (box >> 1) & 1, box & 1


def own_pairs_body(pts_ref, tst_ref, out_ref, left_ref, base_ref, slope_ref):
    for b in range(8):
        put_left(pts_ref[b], left_ref, b)
        put_right(pts_ref[b], base_ref, slope_ref, b)
        out_ref[b] = jnp.zeros((S, N), F32)

    def square(n, b):
        nx, ny, nz = bits(n)
        bx, by, bz = bits(b)
        return square_tile(left_ref[n], base_ref[b], slope_ref[b], (nx - bx, ny - by, nz - bz))

    def use(n, b, both, tile):
        out_ref[b] = out_ref[b] + jnp.dot(tst_ref[n], tile, preferred_element_type=F32)
        if both:
            out_ref[n] = out_ref[n] + lax.dot_general(
                tst_ref[b], tile, (((1,), (1,)), ((), ())), preferred_element_type=F32
            )

    def step(i, carry):
        pairs = [
            ((first + shift) & 7, first, shift > 0) for first in (i, i + 4) for shift in range(4)
        ]
        pairs.append((i + 4, i, True))
        pipelined(
            [functools.partial(square, n, b) for n, b, _ in pairs],
            [functools.partial(use, n, b, both) for n, b, both in pairs],
        )
        return carry

    lax.fori_loop(0, 4, step, 0)


def vmem(shape, dtype):
    return pltpu.VMEM(shape, dtype)


def near(value):
    return pltpu.with_memory_space_constraint(value, pltpu.VMEM)


def own_pairs(points, tests):
    return pl.pallas_call(
        own_pairs_body,
        out_shape=vmem((8, S, N), F32),
        scratch_shapes=[
            vmem((8, N, FEAT), BF16),
            vmem((8, FEAT, N), F32),
            vmem((8, FEAT, N), F32),
        ],
        name="own_pairs",
    )(points, tests)


def halo_tiles(jobs, own, part_ref, out_ref, left_ref, halo_ref, base_ref, slope_ref):
    totals = [part_ref[own + bz] for bz in range(2)]

    def square(slot, box, bz, off):
        return square_tile(left_ref[slot], base_ref[own + bz], slope_ref[own + bz], off)

    def use(slot, box, bz, off, tile):
        tests = halo_ref[box, :S, :]
        totals[bz] = totals[bz] + jnp.dot(tests, tile, preferred_element_type=F32)

    pipelined(
        [functools.partial(square, *job) for job in jobs],
        [functools.partial(use, *job) for job in jobs],
    )
    for bz in range(2):
        out_ref[own + bz] = totals[bz]


def halo_prep(pts_ref, sides, left_ref, base_ref, slope_ref):
    count = sides[0].shape[0]
    for side, ref in enumerate(sides):
        for box in range(count):
            put_left(ref[box, S : S + 3, :], left_ref, side * count + box)
    for b in range(8):
        put_right(pts_ref[b], base_ref, slope_ref, b)


def halo_x_body(pts_ref, low_ref, high_ref, part_ref, out_ref, left_ref, base_ref, slope_ref):
    sides = (low_ref, high_ref)
    halo_prep(pts_ref, sides, left_ref, base_ref, slope_ref)
    for i, side in enumerate(sides):

        def step(j, carry):
            jobs = [
                (i * 4 + ny * 2 + nz, ny * 2 + nz, bz, (2 * i - 1, ny - j, nz - bz))
                for bz in range(2) for ny in range(2) for nz in range(2)
            ]
            halo_tiles(
                jobs, i * 4 + j * 2, part_ref, out_ref, left_ref, side, base_ref, slope_ref
            )
            return carry

        lax.fori_loop(0, 2, step, 0)


def halo_x(points, low, high, part):
    return pl.pallas_call(
        halo_x_body,
        out_shape=vmem((8, S, N), F32),
        in_specs=[vmem_spec()] * 4,
        scratch_shapes=[
            vmem((8, N, FEAT), BF16),
            vmem((8, FEAT, N), F32),
            vmem((8, FEAT, N), F32),
        ],
        name="halo_x",
    )(points, near(low), near(high), near(part))


def spread_row(block, row):
    return jnp.broadcast_to(block[row : row + 1, :], block.shape)


def minus(blocks, mults, row):
    return [b - m * row for b, m in zip(blocks, mults)]


def eliminate(groups, lane_of, panel):
    groups = [[list(blocks) for blocks in group] for group in groups]
    sub = lax.broadcasted_iota(jnp.int32, (8, 128), 0)
    for kb in range(8):
        diags = [jnp.ones((8, 128), F32) for _ in groups]
        for start in range(0, 8, panel):
            lanes = [lane_of(kb * 8 + start + j) for j in range(panel)]
            panels = [
                [
                    [jnp.take_along_axis(group[0][r], lane, axis=1) for r in range(kb, 8)]
                    for lane in lanes
                ]
                for group in groups
            ]
            for j in range(0, panel, 2):
                s = start + j
                for p, (group, cols) in enumerate(zip(groups, panels)):
                    one, two = cols[j], cols[j + 1]
                    a00 = spread_row(one[0], s)
                    a01 = spread_row(two[0], s)
                    a11 = spread_row(two[0], s + 1)
                    root0 = lax.rsqrt(a00)
                    root1 = lax.rsqrt(a00 * a11 - a01 * a01)
                    inv0 = root0 * root0
                    inv1 = (root1 * root1) * a00
                    m0 = [c * inv0 for c in one]
                    m0[0] = jnp.where(sub > s, m0[0], 0.0)
                    two = minus(two, m0, a01)
                    m1 = [c * inv1 for c in two]
                    m1[0] = jnp.where(sub > s + 1, m1[0], 0.0)
                    diags[p] = jnp.where(
                        sub == s, one[0], jnp.where(sub == s + 1, two[0], diags[p])
                    )
                    for jj in range(j + 2, panel):
                        cols[jj] = minus(cols[jj], m0, spread_row(cols[jj][0], s))
                        cols[jj] = minus(cols[jj], m1, spread_row(cols[jj][0], s + 1))
                    for blocks in group:
                        blocks[kb:] = minus(blocks[kb:], m0, spread_row(blocks[kb], s))
                        blocks[kb:] = minus(blocks[kb:], m1, spread_row(blocks[kb], s + 1))
        for p, group in enumerate(groups):
            root = lax.rsqrt(diags[p])
            for blocks in group:
                blocks[kb] = blocks[kb] * root
    return groups


def row_blocks(value):
    return [value[r * 8 : r * 8 + 8, :] for r in range(8)]


def total(value):
    return jnp.sum(jnp.sum(value, axis=0, keepdims=True), axis=1, keepdims=True)


def factor_one(gram, rank):
    row = lax.broadcasted_iota(jnp.int32, (S, S), 0)
    col = lax.broadcasted_iota(jnp.int32, (S, S), 1)
    eye = row == col
    trace = total(jnp.where(eye, gram, 0.0))
    shift = SHIFT_SHARE * trace / S + TINY
    shifted = gram + jnp.where(eye, shift, 0.0)
    both = jnp.concatenate([shifted, jnp.where(eye, 1.0, 0.0).astype(F32)], axis=1)
    done = eliminate(
        [[row_blocks(both)]], lambda k: jnp.full((8, 128), k, jnp.int32), ONE_PANEL
    )
    both = jnp.concatenate(done[0][0], axis=0)
    inverse = both[:, S:]
    upper = jnp.where(col >= row, both[:, :S], 0.0)
    projected = jnp.where(row < rank, upper - shift * inverse, 0.0)
    return inverse, projected, trace


def factor_pairs(grams, rank):
    row = lax.broadcasted_iota(jnp.int32, (S, 128), 0)
    lane = lax.broadcasted_iota(jnp.int32, (S, 128), 1)
    first = lane < S
    col = lane & (S - 1)
    eye = row == col
    ident = jnp.where(eye, 1.0, 0.0).astype(F32)
    half = lax.broadcasted_iota(jnp.int32, (8, 128), 1) & S
    shifts, groups = [], []
    for gram in grams:
        packed = jnp.where(first, gram[:S], gram[S:])
        diag = jnp.where(eye, packed, 0.0)
        traces = total(jnp.where(first, diag, 0.0)), total(jnp.where(first, 0.0, diag))
        shift = [SHIFT_SHARE * t / S + TINY for t in traces]
        shift = jnp.where(first, shift[0], shift[1])
        shifts.append(shift)
        groups.append([row_blocks(packed + jnp.where(eye, shift, 0.0)), row_blocks(ident)])
    out = []
    for shift, (left, right) in zip(shifts, eliminate(groups, lambda k: half + k, LEAF_PANEL)):
        inverse = jnp.concatenate(right, axis=0)
        upper = jnp.where(col >= row, jnp.concatenate(left, axis=0), 0.0)
        out.append((inverse, jnp.where(row < rank, upper - shift * inverse, 0.0)))
    return out


def gram_of(rows):
    return lax.dot_general(
        rows, rows, (((0,), (0,)), ((), ())), precision=HIGH, preferred_element_type=F32
    )


def times_t(a, b):
    return lax.dot_general(
        a, b, (((1,), (1,)), ((), ())), precision=HIGH, preferred_element_type=F32
    )


def keep_first(value, rank):
    row = lax.broadcasted_iota(jnp.int32, value.shape, value.ndim - 2)
    return jnp.where(row < rank, value, 0.0)


def halo_y_body(
    rank_ref, pts_ref, low_ref, high_ref, part_ref,
    sample_ref, inv_ref, proj_ref, inv1_ref, cur_ref, gram_ref,
    left_ref, base_ref, slope_ref,
):
    sides = (low_ref, high_ref)
    halo_prep(pts_ref, sides, left_ref, base_ref, slope_ref)
    for j, side in enumerate(sides):

        def step(i, carry):
            jobs = [
                (j * 8 + (i + dx) * 2 + nz, (i + dx) * 2 + nz, bz, (dx - 1, 2 * j - 1, nz - bz))
                for bz in range(2) for dx in range(3) for nz in range(2)
            ]
            halo_tiles(
                jobs, i * 4 + j * 2, part_ref, sample_ref, left_ref, side, base_ref, slope_ref
            )
            return carry

        lax.fori_loop(0, 2, step, 0)
    leaf_factor(rank_ref, sample_ref, inv_ref, proj_ref, inv1_ref, cur_ref, gram_ref)


def leaf_factor(rank_ref, sample_ref, inv_ref, proj_ref, inv1_ref, cur_ref, gram_ref):
    def group(g, carry):
        first = g * (2 * LEAF_PAIRS)
        grams = []
        for p in range(LEAF_PAIRS):
            pair = jnp.concatenate([sample_ref[first + 2 * p + k] for k in range(2)], axis=0)
            grams.append(times_t(pair, pair))
        for p, (inverse, projected) in enumerate(factor_pairs(grams, rank_ref[0])):
            for k in range(2):
                inv_ref[first + 2 * p + k] = inverse[:, k * S : k * S + S]
                proj_ref[first + 2 * p + k] = projected[:, k * S : k * S + S]
        return carry

    lax.fori_loop(0, 4 // LEAF_PAIRS, group, 0)
    gram = gram_of(proj_ref[...].reshape(8 * S, S))
    inverse, current, _ = factor_one(gram, rank_ref[1])
    inv1_ref[...] = inverse
    cur_ref[...] = current
    gram_ref[...] = gram_of(current)


def smem_spec():
    return pl.BlockSpec(memory_space=pltpu.SMEM)


def vmem_spec():
    return pl.BlockSpec(memory_space=pltpu.VMEM)


def halo_y(ranks, points, low, high, part):
    small = vmem((S, S), F32)
    many = vmem((8, S, S), F32)
    return pl.pallas_call(
        halo_y_body,
        out_shape=(vmem((8, S, N), F32), many, many, small, small, small),
        in_specs=[smem_spec()] + [vmem_spec()] * 4,
        scratch_shapes=[
            vmem((16, N, FEAT), BF16),
            vmem((8, FEAT, N), F32),
            vmem((8, FEAT, N), F32),
        ],
        name="halo_y",
    )(ranks, points, near(low), near(high), near(part))


def transfer_of(inverse, current, rank):
    return keep_first(times_t(inverse, current), rank) * math.sqrt(S)


def upper_body(height, rank_ref, g0, g1, g2, g3, *refs):
    gram = (g0[...] + g1[...]) + (g2[...] + g3[...])
    rank = rank_ref[height]
    if height == 2:
        inv1_in, proj_in, inv_ref, cur_ref, gram_ref, leaf_ref = refs
        for b in range(8):
            leaf_ref[b] = transfer_of(inv1_in[...], proj_in[b], rank_ref[1])
    elif height == 3:
        inv_in, cur_in, leaf_in, sample_in, inv_ref, cur_ref, gram_ref, done_ref, basis_ref = refs
        done_ref[...] = transfer_of(inv_in[...], cur_in[...], rank_ref[2])
        for b in range(8):
            basis = jnp.dot(leaf_in[b], sample_in[b], precision=HIGH, preferred_element_type=F32)
            basis_ref[b] = (keep_first(basis, rank_ref[0]) * math.sqrt(N)).astype(BF16)
    else:
        inv_in, cur2_in, cur_in, done_in, upper_ref, top_ref = refs
        upper_ref[0] = done_in[...]
        upper_ref[1] = transfer_of(inv_in[...], cur2_in[...], rank_ref[3])
    inverse, current, trace = factor_one(gram, rank)
    if height == 4:
        upper_ref[2] = transfer_of(inverse, cur_in[...], rank)
        top_ref[...] = current / jnp.sqrt(trace / S + TINY)
        return
    inv_ref[...] = inverse
    cur_ref[...] = current
    gram_ref[...] = gram_of(current)


def upper(height, ranks, grams, extra):
    small = vmem((S, S), F32)
    out = {
        2: (small,) * 3 + (jax.ShapeDtypeStruct((8, S, S), F32),),
        3: (small,) * 4 + (jax.ShapeDtypeStruct((8, S, N), BF16),),
        4: (jax.ShapeDtypeStruct((3, S, S), F32), jax.ShapeDtypeStruct((S, S), F32)),
    }[height]

    def body(*refs):
        upper_body(height, *refs)

    return pl.pallas_call(
        body,
        out_shape=out,
        in_specs=[smem_spec()] + [vmem_spec()] * (4 + len(extra)),
        name="upper" + str(height),
    )(ranks, *(near(value) for value in (*grams, *extra)))


def shift_pair(head, tail, axis):
    count = lax.axis_size(axis)
    up = [(i, i + 1) for i in range(count - 1)]
    down = [(i + 1, i) for i in range(count - 1)]
    return lax.ppermute(tail, axis, up), lax.ppermute(head, axis, down)


def siblings(value, flip_leaf, flip_brick):
    rows, cols = lax.axis_size("leaf"), lax.axis_size("brick")
    out = [value]
    for dx, dy in ((0, flip_brick), (flip_leaf, 0), (flip_leaf, flip_brick)):
        perm = [
            (i * cols + j, (i ^ dx) * cols + (j ^ dy)) for i in range(rows) for j in range(cols)
        ]
        out.append(lax.ppermute(value, ("leaf", "brick"), perm))
    return out


def shards(points, test_matrix, trunc_ranks):
    packed = jnp.concatenate([test_matrix, points], axis=3)
    rows = S + 3
    own_points = points.reshape(8, 3, N)
    own_tests = test_matrix.reshape(8, S, N)
    low, high = shift_pair(packed[:1], packed[1:], "leaf")
    part = own_pairs(own_points, own_tests)
    low, high, part = lax.optimization_barrier((low, high, part))
    wide = [low, packed, high]
    south = jnp.concatenate([w[:, :1] for w in wide], axis=0)
    north = jnp.concatenate([w[:, 1:] for w in wide], axis=0)
    below, above = shift_pair(south, north, "brick")
    part = halo_x(own_points, low.reshape(4, rows, N), high.reshape(4, rows, N), part)
    sample, inverse, projected, inverse1, current1, gram = halo_y(
        trunc_ranks, own_points, below.reshape(8, rows, N), above.reshape(8, rows, N), part
    )
    inverse2, current2, gram, transfer = upper(
        2, trunc_ranks, siblings(gram, 1, 1), (inverse1, projected)
    )
    inverse3, current3, gram, done2, basis = upper(
        3, trunc_ranks, siblings(gram, 3, 2), (inverse2, current1, inverse, sample)
    )
    uppers, top = upper(
        4, trunc_ranks, siblings(gram, 4, 4), (inverse3, current2, current3, done2)
    )
    block = points.shape[:3]
    return (
        basis.reshape(block + (S, N)),
        transfer.reshape(block + (S, S)),
        uppers[:, None, None],
        top[None, None],
    )


def solution(mesh):
    placed = (P("leaf", "brick", None, None, None), P("leaf", "brick", None, None, None), P())
    return jax.shard_map(
        shards,
        mesh=mesh,
        in_specs=placed,
        out_specs=(
            P("leaf", "brick", None, None, None),
            P("leaf", "brick", None, None, None),
            P(None, "leaf", "brick", None, None),
            P("leaf", "brick", None, None),
        ),
        check_vma=False,
    )
```

time: 314 us -> 89.6 us (0.29)
  the two profiles are of different devices: /device:TPU:152 before, /device:TPU:128 now
where the time goes in v1:
time: 89.6 us; the launch traced here: 88.7 us
  starting transfers between devices  45.2 us (50%)
  Pallas kernels  30.6 us (34%)
  waiting for transfers between devices  10.3 us (11%)
  local copies, waits for them, and re-layouts  1.66 us (2%)
    ppermute x9, starting transfers between devices, siblings(): out.append(lax.ppermute(value, ('leaf', 'brick'), perm))  36.8 us
    pallas_call x1, Pallas kernels, halo_y(): pl.pallas_call(halo_y_body, out_shape=(vmem((8, S, N), F32), many, many,...  11.5 us
    ppermute x9, waiting for transfers between devices, siblings(): out.append(lax.ppermute(value, ('leaf', 'brick'), perm))  8.87 us
    pallas_call x3, Pallas kernels, upper(): pl.pallas_call(body, out_shape=out, in_specs=[smem_spec()] + [vmem_spec()...  8.51 us
    ppermute x4, starting transfers between devices, shift_pair(): return (lax.ppermute(tail, axis, up), lax.ppermute(head, axis, down))  8.44 us
    pallas_call x1, Pallas kernels, own_pairs(): pl.pallas_call(own_pairs_body, out_shape=vmem((8, S, N), F32), scratch_sh...  5.74 us
    pallas_call x1, Pallas kernels, halo_x(): pl.pallas_call(halo_x_body, out_shape=vmem((8, S, N), F32), in_specs=[vme...  4.87 us
  transfers between devices with their start and end apart: 13, of which 6 were waited for; matrix products, arithmetic and copies ran while one was open for 0% of the time, Pallas kernels for 12%

profile of v1, /device:TPU:128, one launch (start us, length us, event | category | flops | bytes accessed | tf_op | source)
XLA Modules:
  0.0 88.7 jit_solution(559945510204058333)
XLA Ops:
  0.6 1.0 %constant_dynamic-update-slice_fusion.1 = bf16[2,2,2,67,256]{4,3,2,1,0:T(8,128)(2,1)S(1)} fusion(bf16[2,2,2,64,256]{4,3,2,1,0:T(8,128)(2,1)} %param.4), kind=kLoop, calls=%fused_computation.3 | loop fusion | bytes 524288
  1.6 0.6 constant_dynamic-update-slice_fusion
  2.3 3.8 %collective-permute-start.1 = (bf16[1,2,2,67,256]{4,3,2,1,0:T(8,128)(2,1)S(1)}, bf16[1,2,2,67,256]{4,3,2,1,0:T(8,128)(2,1)S(1)}, u32[]{:S(2)}, u32[]{:S(2)}) collective-permute-start(bf16[1,2,2,67,256]{4,3,2,1,0:T(8,128)(2,1)S(1)} %get-tuple-element.50), channel_id=1, source_target_pairs={{16,0},{32,16},{48,32},{64,48},{80,64},{96,80},{112,96},{128,112},... | collective-permute-start | bytes 411656 | tf_op jit(solution)/shard_map/ppermute | solution.py:463
  6.0 2.1 %collective-permute-start = (bf16[1,2,2,67,256]{4,3,2,1,0:T(8,128)(2,1)S(1)}, bf16[1,2,2,67,256]{4,3,2,1,0:T(8,128)(2,1)S(1)}, u32[]{:S(2)}, u32[]{:S(2)}) collective-permute-start(bf16[1,2,2,67,256]{4,3,2,1,0:T(8,128)(2,1)S(1)} %get-tuple-element.51), channel_id=1, source_target_pairs={{0,16},{16,32},{32,48},{48,64},{64,80},{80,96},{96,112},{112,128},... | collective-permute-start | bytes 411656 | tf_op jit(solution)/shard_map/ppermute | solution.py:463
  8.1 5.7 %own_pairs.1.part_ref = f32[8,64,256]{2,1,0:T(8,128)S(1)} custom-call(bf16[8,3,256]{2,1,0:T(4,128)(2,1)} %bitcast.17, bf16[8,64,256]{2,1,0:T(8,128)(2,1)} %bitcast.16), custom_call_target="tpu_custom_call" | custom-call | tf_op jit(solution)/shard_map/own_pairs/pallas_call | solution.py:148
  13.9 0.0 collective-permute-done.1
  13.9 1.4 %collective-permute-done = bf16[1,2,2,67,256]{4,3,2,1,0:T(8,128)(2,1)S(1)} collective-permute-done((bf16[1,2,2,67,256]{4,3,2,1,0:T(8,128)(2,1)S(1)}, bf16[1,2,2,67,256]{4,3,2,1,0:T(8,128)(2,1)S(1)}, u32[]{:S(2)}, u32[]{:S(2)}) %collective-permute-start) | collective-permute-done | bytes 137248 | tf_op jit(solution)/shard_map/ppermute | solution.py:463
  15.4 1.3 %collective-permute-start.2 = (bf16[4,1,2,67,256]{4,3,2,1,0:T(8,128)(2,1)S(1)}, bf16[4,1,2,67,256]{4,3,2,1,0:T(8,128)(2,1)S(1)}, u32[]{:S(2)}, u32[]{:S(2)}) collective-permute-start(bf16[4,1,2,67,256]{4,3,2,1,0:T(8,128)(2,1)S(1)} %pad_maximum_fusion), channel_id=1, source_target_pairs={{0,1},{1,2},{2,3},{3,4},{4,5},{5,6},{6,7},{7,8},{8,9},{9,10},{10,1... | collective-permute-start | bytes 823304 | tf_op jit(solution)/shard_map/ppermute | solution.py:463
  16.8 1.3 %collective-permute-start.3 = (bf16[4,1,2,67,256]{4,3,2,1,0:T(8,128)(2,1)S(1)}, bf16[4,1,2,67,256]{4,3,2,1,0:T(8,128)(2,1)S(1)}, u32[]{:S(2)}, u32[]{:S(2)}) collective-permute-start(bf16[4,1,2,67,256]{4,3,2,1,0:T(8,128)(2,1)S(1)} %pad_maximum_fusion.1), channel_id=1, source_target_pairs={{1,0},{2,1},{3,2},{4,3},{5,4},{6,5},{7,6},{8,7},{9,8},{10,9},{11,1... | collective-permute-start | bytes 823304 | tf_op jit(solution)/shard_map/ppermute | solution.py:463
  18.1 4.9 %halo_x.1.part_ref = f32[8,64,256]{2,1,0:T(8,128)S(1)} custom-call(bf16[8,3,256]{2,1,0:T(4,128)(2,1)} %bitcast.18, bf16[4,67,256]{2,1,0:T(8,128)(2,1)S(1)} %bitcast.13, bf16[4,67,256]{2,1,0:T(8,128)(2,1)S(1)} %bitcast.12, f32[8,64,256]{2,1,0:T(8,128)S(1)} %own_pairs.1.part_ref), custom_call_target="tpu_custom_call" | custom-call | tf_op jit(solution)/shard_map/halo_x/pallas_call | solution.py:206
  23.0 0.0 collective-permute-done.2
  23.0 0.0 collective-permute-done.3
  23.0 11.5 %halo_y.1 = (f32[8,64,256]{2,1,0:T(8,128)S(1)}, f32[8,64,64]{2,1,0:T(8,128)S(1)}, f32[8,64,64]{2,1,0:T(8,128)S(1)}, f32[64,64]{1,0:T(8,128)S(1)}, f32[64,64]{1,0:T(8,128)S(1)}, /*index=5*/f32[64,64]{1,0:T(8,128)S(1)}) custom-call(s32[5]{0:T(128)} %refs_0_.5, bf16[8,3,256]{2,1,0:T(4,128)(2,1)} %bitcast.19, bf16[8,67,256]{2,1,0:T(8,128)(2,1)S(1)} %bitcast.14, ...), custom_call_target="tpu_custom_call" | custom-call | tf_op jit(solution)/shard_map/halo_y/pallas_call | solution.py:396
  34.5 5.7 %collective-permute-start.6 = (f32[64,64]{1,0:T(8,128)S(1)}, f32[64,64]{1,0:T(8,128)S(1)}, u32[]{:S(2)}, u32[]{:S(2)}) collective-permute-start(f32[64,64]{1,0:T(8,128)S(1)} %get-tuple-element.27.refs_1_), channel_id=1, source_target_pairs={{0,17},{1,16},{2,19},{3,18},{4,21},{5,20},{6,23},{7,22},{8,25},{9,... | collective-permute-start | bytes 49160 | tf_op jit(solution)/shard_map/ppermute | solution.py:473
  40.2 3.9 %collective-permute-start.5 = (f32[64,64]{1,0:T(8,128)S(1)}, f32[64,64]{1,0:T(8,128)S(1)}, u32[]{:S(2)}, u32[]{:S(2)}) collective-permute-start(f32[64,64]{1,0:T(8,128)S(1)} %get-tuple-element.27.refs_1_), channel_id=1, source_target_pairs={{0,16},{1,17},{2,18},{3,19},{4,20},{5,21},{6,22},{7,23},{8,24},{9,... | collective-permute-start | bytes 49160 | tf_op jit(solution)/shard_map/ppermute | solution.py:473
  44.1 2.1 %collective-permute-start.4 = (f32[64,64]{1,0:T(8,128)S(1)}, f32[64,64]{1,0:T(8,128)S(1)}, u32[]{:S(2)}, u32[]{:S(2)}) collective-permute-start(f32[64,64]{1,0:T(8,128)S(1)} %get-tuple-element.27.refs_1_), channel_id=1, source_target_pairs={{0,1},{1,0},{2,3},{3,2},{4,5},{5,4},{6,7},{7,6},{8,9},{9,8},{10,11... | collective-permute-start | bytes 49160 | tf_op jit(solution)/shard_map/ppermute | solution.py:473
  46.2 0.0 collective-permute-done.5.refs_3_
  46.2 1.0 %collective-permute-done.4.refs_2_ = f32[64,64]{1,0:T(8,128)S(1)} collective-permute-done((f32[64,64]{1,0:T(8,128)S(1)}, f32[64,64]{1,0:T(8,128)S(1)}, u32[]{:S(2)}, u32[]{:S(2)}) %collective-permute-start.4) | collective-permute-done | bytes 16416 | tf_op jit(solution)/shard_map/ppermute | solution.py:473
  47.2 2.8 %upper2.1 = (f32[64,64]{1,0:T(8,128)S(1)}, f32[64,64]{1,0:T(8,128)S(1)}, f32[64,64]{1,0:T(8,128)S(1)}, f32[8,64,64]{2,1,0:T(8,128)}) custom-call(s32[5]{0:T(128)} %refs_0_.5, f32[64,64]{1,0:T(8,128)S(1)} %get-tuple-element.27.refs_1_, f32[64,64]{1,0:T(8,128)S(1)} %collective-permute-done.4.refs_2_, f32[64,64]{1,0:T(8,128)S(1)} %collective-permute-done.5.refs_3_, ...), custom_call_target="tpu_custom_call" | custom-call | tf_op jit(solution)/shard_map/upper2/pallas_call | solution.py:451
  49.9 6.4 %collective-permute-start.9 = (f32[64,64]{1,0:T(8,128)S(1)}, f32[64,64]{1,0:T(8,128)S(1)}, u32[]{:S(2)}, u32[]{:S(2)}) collective-permute-start(f32[64,64]{1,0:T(8,128)S(1)} %get-tuple-element.30.refs_1_), channel_id=1, source_target_pairs={{0,50},{1,51},{2,48},{3,49},{4,54},{5,55},{6,52},{7,53},{8,58},{9,... | collective-permute-start | bytes 49160 | tf_op jit(solution)/shard_map/ppermute | solution.py:473
  56.3 1.9 %collective-permute-start.8 = (f32[64,64]{1,0:T(8,128)S(1)}, f32[64,64]{1,0:T(8,128)S(1)}, u32[]{:S(2)}, u32[]{:S(2)}) collective-permute-start(f32[64,64]{1,0:T(8,128)S(1)} %get-tuple-element.30.refs_1_), channel_id=1, source_target_pairs={{0,48},{1,49},{2,50},{3,51},{4,52},{5,53},{6,54},{7,55},{8,56},{9,... | collective-permute-start | bytes 49160 | tf_op jit(solution)/shard_map/ppermute | solution.py:473
  58.2 2.5 %collective-permute-start.7 = (f32[64,64]{1,0:T(8,128)S(1)}, f32[64,64]{1,0:T(8,128)S(1)}, u32[]{:S(2)}, u32[]{:S(2)}) collective-permute-start(f32[64,64]{1,0:T(8,128)S(1)} %get-tuple-element.30.refs_1_), channel_id=1, source_target_pairs={{0,2},{1,3},{2,0},{3,1},{4,6},{5,7},{6,4},{7,5},{8,10},{9,11},{10,... | collective-permute-start | bytes 49160 | tf_op jit(solution)/shard_map/ppermute | solution.py:473
  60.7 2.6 %collective-permute-done.8.refs_3_ = f32[64,64]{1,0:T(8,128)S(1)} collective-permute-done((f32[64,64]{1,0:T(8,128)S(1)}, f32[64,64]{1,0:T(8,128)S(1)}, u32[]{:S(2)}, u32[]{:S(2)}) %collective-permute-start.8) | collective-permute-done | bytes 16416 | tf_op jit(solution)/shard_map/ppermute | solution.py:473
  63.3 0.7 collective-permute-done.7.refs_2_
  64.0 2.9 %upper3.1 = (f32[64,64]{1,0:T(8,128)S(1)}, f32[64,64]{1,0:T(8,128)S(1)}, f32[64,64]{1,0:T(8,128)S(1)}, f32[64,64]{1,0:T(8,128)S(1)}, bf16[8,64,256]{2,1,0:T(8,128)(2,1)}) custom-call(s32[5]{0:T(128)} %refs_0_.5, f32[64,64]{1,0:T(8,128)S(1)} %get-tuple-element.30.refs_1_, f32[64,64]{1,0:T(8,128)S(1)} %collective-permute-done.7.refs_2_, ...), custom_call_target="tpu_custom_call" | custom-call | tf_op jit(solution)/shard_map/upper3/pallas_call | solution.py:451
  66.9 9.9 %collective-permute-start.12 = (f32[64,64]{1,0:T(8,128)S(1)}, f32[64,64]{1,0:T(8,128)S(1)}, u32[]{:S(2)}, u32[]{:S(2)}) collective-permute-start(f32[64,64]{1,0:T(8,128)S(1)} %get-tuple-element.37.refs_1_), channel_id=1, source_target_pairs={{0,68},{1,69},{2,70},{3,71},{4,64},{5,65},{6,66},{7,67},{8,76},{9,... | collective-permute-start | bytes 49160 | tf_op jit(solution)/shard_map/ppermute | solution.py:473
  76.8 1.9 %collective-permute-start.11 = (f32[64,64]{1,0:T(8,128)S(1)}, f32[64,64]{1,0:T(8,128)S(1)}, u32[]{:S(2)}, u32[]{:S(2)}) collective-permute-start(f32[64,64]{1,0:T(8,128)S(1)} %get-tuple-element.37.refs_1_), channel_id=1, source_target_pairs={{0,64},{1,65},{2,66},{3,67},{4,68},{5,69},{6,70},{7,71},{8,72},{9,... | collective-permute-start | bytes 49160 | tf_op jit(solution)/shard_map/ppermute | solution.py:473
  78.8 2.5 %collective-permute-start.10 = (f32[64,64]{1,0:T(8,128)S(1)}, f32[64,64]{1,0:T(8,128)S(1)}, u32[]{:S(2)}, u32[]{:S(2)}) collective-permute-start(f32[64,64]{1,0:T(8,128)S(1)} %get-tuple-element.37.refs_1_), channel_id=1, source_target_pairs={{0,4},{1,5},{2,6},{3,7},{4,0},{5,1},{6,2},{7,3},{8,12},{9,13},{10,... | collective-permute-start | bytes 49160 | tf_op jit(solution)/shard_map/ppermute | solution.py:473
  81.3 0.0 collective-permute-done.12.refs_4_
  81.3 1.4 %collective-permute-done.11.refs_3_ = f32[64,64]{1,0:T(8,128)S(1)} collective-permute-done((f32[64,64]{1,0:T(8,128)S(1)}, f32[64,64]{1,0:T(8,128)S(1)}, u32[]{:S(2)}, u32[]{:S(2)}) %collective-permute-start.11) | collective-permute-done | bytes 16416 | tf_op jit(solution)/shard_map/ppermute | solution.py:473
  82.7 3.2 %collective-permute-done.10.refs_2_ = f32[64,64]{1,0:T(8,128)S(1)} collective-permute-done((f32[64,64]{1,0:T(8,128)S(1)}, f32[64,64]{1,0:T(8,128)S(1)}, u32[]{:S(2)}, u32[]{:S(2)}) %collective-permute-start.10) | collective-permute-done | bytes 16416 | tf_op jit(solution)/shard_map/ppermute | solution.py:473
  85.8 2.9 %upper4.1 = (f32[3,64,64]{2,1,0:T(8,128)}, f32[64,64]{1,0:T(8,128)}) custom-call(s32[5]{0:T(128)} %refs_0_.5, f32[64,64]{1,0:T(8,128)S(1)} %get-tuple-element.37.refs_1_, f32[64,64]{1,0:T(8,128)S(1)} %collective-permute-done.10.refs_2_, f32[64,64]{1,0:T(8,128)S(1)} %collective-permute-done.11.refs_3_, f32[64,64]{1,0:T(8,128)S(1)} %collective-permute-done.12.refs_4_, ...), custom_call_target="tpu_custom_call" | custom-call | tf_op jit(solution)/shard_map/upper4/pallas_call | solution.py:451
  (9 shorter events, 0.1 us)
Async XLA Ops:
  0.6 1.0 %copy-start = (bf16[2,2,2,3,256]{4,2,3,1,0:T(2,128)(2,1)S(1)}, bf16[2,2,2,3,256]{4,2,3,1,0:T(2,128)(2,1)}, u32[]{:S(2)}) copy-start(bf16[2,2,2,3,256]{4,2,3,1,0:T(2,128)(2,1)} %param.3) | copy-start | bytes 36868
  2.3 11.6 %collective-permute-start.1 = (bf16[1,2,2,67,256]{4,3,2,1,0:T(8,128)(2,1)S(1)}, bf16[1,2,2,67,256]{4,3,2,1,0:T(8,128)(2,1)S(1)}, u32[]{:S(2)}, u32[]{:S(2)}) collective-permute-start(bf16[1,2,2,67,256]{4,3,2,1,0:T(8,128)(2,1)S(1)} %get-tuple-element.50), channel_id=1, source_target_pairs={{16,0},{32,16},{48,32},{64,48},{80,64},{96,80},{112,96},{128,112},... | collective-permute-start | bytes 411656 | tf_op jit(solution)/shard_map/ppermute | solution.py:463
  6.0 9.3 %collective-permute-start = (bf16[1,2,2,67,256]{4,3,2,1,0:T(8,128)(2,1)S(1)}, bf16[1,2,2,67,256]{4,3,2,1,0:T(8,128)(2,1)S(1)}, u32[]{:S(2)}, u32[]{:S(2)}) collective-permute-start(bf16[1,2,2,67,256]{4,3,2,1,0:T(8,128)(2,1)S(1)} %get-tuple-element.51), channel_id=1, source_target_pairs={{0,16},{16,32},{32,48},{48,64},{64,80},{80,96},{96,112},{112,128},... | collective-permute-start | bytes 411656 | tf_op jit(solution)/shard_map/ppermute | solution.py:463
  15.4 7.5 %collective-permute-start.2 = (bf16[4,1,2,67,256]{4,3,2,1,0:T(8,128)(2,1)S(1)}, bf16[4,1,2,67,256]{4,3,2,1,0:T(8,128)(2,1)S(1)}, u32[]{:S(2)}, u32[]{:S(2)}) collective-permute-start(bf16[4,1,2,67,256]{4,3,2,1,0:T(8,128)(2,1)S(1)} %pad_maximum_fusion), channel_id=1, source_target_pairs={{0,1},{1,2},{2,3},{3,4},{4,5},{5,6},{6,7},{7,8},{8,9},{9,10},{10,1... | collective-permute-start | bytes 823304 | tf_op jit(solution)/shard_map/ppermute | solution.py:463
  16.8 6.2 %collective-permute-start.3 = (bf16[4,1,2,67,256]{4,3,2,1,0:T(8,128)(2,1)S(1)}, bf16[4,1,2,67,256]{4,3,2,1,0:T(8,128)(2,1)S(1)}, u32[]{:S(2)}, u32[]{:S(2)}) collective-permute-start(bf16[4,1,2,67,256]{4,3,2,1,0:T(8,128)(2,1)S(1)} %pad_maximum_fusion.1), channel_id=1, source_target_pairs={{1,0},{2,1},{3,2},{4,3},{5,4},{6,5},{7,6},{8,7},{9,8},{10,9},{11,1... | collective-permute-start | bytes 823304 | tf_op jit(solution)/shard_map/ppermute | solution.py:463
  34.5 11.7 %collective-permute-start.6 = (f32[64,64]{1,0:T(8,128)S(1)}, f32[64,64]{1,0:T(8,128)S(1)}, u32[]{:S(2)}, u32[]{:S(2)}) collective-permute-start(f32[64,64]{1,0:T(8,128)S(1)} %get-tuple-element.27.refs_1_), channel_id=1, source_target_pairs={{0,17},{1,16},{2,19},{3,18},{4,21},{5,20},{6,23},{7,22},{8,25},{9,... | collective-permute-start | bytes 49160 | tf_op jit(solution)/shard_map/ppermute | solution.py:473
  40.2 6.0 %collective-permute-start.5 = (f32[64,64]{1,0:T(8,128)S(1)}, f32[64,64]{1,0:T(8,128)S(1)}, u32[]{:S(2)}, u32[]{:S(2)}) collective-permute-start(f32[64,64]{1,0:T(8,128)S(1)} %get-tuple-element.27.refs_1_), channel_id=1, source_target_pairs={{0,16},{1,17},{2,18},{3,19},{4,20},{5,21},{6,22},{7,23},{8,24},{9,... | collective-permute-start | bytes 49160 | tf_op jit(solution)/shard_map/ppermute | solution.py:473
  44.1 3.1 %collective-permute-start.4 = (f32[64,64]{1,0:T(8,128)S(1)}, f32[64,64]{1,0:T(8,128)S(1)}, u32[]{:S(2)}, u32[]{:S(2)}) collective-permute-start(f32[64,64]{1,0:T(8,128)S(1)} %get-tuple-element.27.refs_1_), channel_id=1, source_target_pairs={{0,1},{1,0},{2,3},{3,2},{4,5},{5,4},{6,7},{7,6},{8,9},{9,8},{10,11... | collective-permute-start | bytes 49160 | tf_op jit(solution)/shard_map/ppermute | solution.py:473
  49.9 10.8 %collective-permute-start.9 = (f32[64,64]{1,0:T(8,128)S(1)}, f32[64,64]{1,0:T(8,128)S(1)}, u32[]{:S(2)}, u32[]{:S(2)}) collective-permute-start(f32[64,64]{1,0:T(8,128)S(1)} %get-tuple-element.30.refs_1_), channel_id=1, source_target_pairs={{0,50},{1,51},{2,48},{3,49},{4,54},{5,55},{6,52},{7,53},{8,58},{9,... | collective-permute-start | bytes 49160 | tf_op jit(solution)/shard_map/ppermute | solution.py:473
  56.3 7.0 %collective-permute-start.8 = (f32[64,64]{1,0:T(8,128)S(1)}, f32[64,64]{1,0:T(8,128)S(1)}, u32[]{:S(2)}, u32[]{:S(2)}) collective-permute-start(f32[64,64]{1,0:T(8,128)S(1)} %get-tuple-element.30.refs_1_), channel_id=1, source_target_pairs={{0,48},{1,49},{2,50},{3,51},{4,52},{5,53},{6,54},{7,55},{8,56},{9,... | collective-permute-start | bytes 49160 | tf_op jit(solution)/shard_map/ppermute | solution.py:473
  58.2 5.8 %collective-permute-start.7 = (f32[64,64]{1,0:T(8,128)S(1)}, f32[64,64]{1,0:T(8,128)S(1)}, u32[]{:S(2)}, u32[]{:S(2)}) collective-permute-start(f32[64,64]{1,0:T(8,128)S(1)} %get-tuple-element.30.refs_1_), channel_id=1, source_target_pairs={{0,2},{1,3},{2,0},{3,1},{4,6},{5,7},{6,4},{7,5},{8,10},{9,11},{10,... | collective-permute-start | bytes 49160 | tf_op jit(solution)/shard_map/ppermute | solution.py:473
  66.9 14.3 %collective-permute-start.12 = (f32[64,64]{1,0:T(8,128)S(1)}, f32[64,64]{1,0:T(8,128)S(1)}, u32[]{:S(2)}, u32[]{:S(2)}) collective-permute-start(f32[64,64]{1,0:T(8,128)S(1)} %get-tuple-element.37.refs_1_), channel_id=1, source_target_pairs={{0,68},{1,69},{2,70},{3,71},{4,64},{5,65},{6,66},{7,67},{8,76},{9,... | collective-permute-start | bytes 49160 | tf_op jit(solution)/shard_map/ppermute | solution.py:473
  76.8 5.8 %collective-permute-start.11 = (f32[64,64]{1,0:T(8,128)S(1)}, f32[64,64]{1,0:T(8,128)S(1)}, u32[]{:S(2)}, u32[]{:S(2)}) collective-permute-start(f32[64,64]{1,0:T(8,128)S(1)} %get-tuple-element.37.refs_1_), channel_id=1, source_target_pairs={{0,64},{1,65},{2,66},{3,67},{4,68},{5,69},{6,70},{7,71},{8,72},{9,... | collective-permute-start | bytes 49160 | tf_op jit(solution)/shard_map/ppermute | solution.py:473
  78.8 7.1 %collective-permute-start.10 = (f32[64,64]{1,0:T(8,128)S(1)}, f32[64,64]{1,0:T(8,128)S(1)}, u32[]{:S(2)}, u32[]{:S(2)}) collective-permute-start(f32[64,64]{1,0:T(8,128)S(1)} %get-tuple-element.37.refs_1_), channel_id=1, source_target_pairs={{0,4},{1,5},{2,6},{3,7},{4,0},{5,1},{6,2},{7,3},{8,12},{9,13},{10,... | collective-permute-start | bytes 49160 | tf_op jit(solution)/shard_map/ppermute | solution.py:473

commit v2 on v1

--- a/solution.py
+++ b/solution.py
@@ -23,6 +23,7 @@
 LEAF_PAIRS = 4
 LEAF_PANEL = 4
 ONE_PANEL = 8
+PAIR_PANEL = 4
 
 
 def split_square(x):
@@ -296,7 +297,7 @@
     return inverse, projected, trace
 
 
-def factor_pairs(grams, rank):
+def factor_pairs(grams, rank, panel):
     row = lax.broadcasted_iota(jnp.int32, (S, 128), 0)
     lane = lax.broadcasted_iota(jnp.int32, (S, 128), 1)
     first = lane < S
@@ -305,8 +306,7 @@
     ident = jnp.where(eye, 1.0, 0.0).astype(F32)
     half = lax.broadcasted_iota(jnp.int32, (8, 128), 1) & S
     shifts, groups = [], []
-    for gram in grams:
-        packed = jnp.where(first, gram[:S], gram[S:])
+    for packed in grams:
         diag = jnp.where(eye, packed, 0.0)
         traces = total(jnp.where(first, diag, 0.0)), total(jnp.where(first, 0.0, diag))
         shift = [SHIFT_SHARE * t / S + TINY for t in traces]
@@ -314,7 +314,7 @@
         shifts.append(shift)
         groups.append([row_blocks(packed + jnp.where(eye, shift, 0.0)), row_blocks(ident)])
     out = []
-    for shift, (left, right) in zip(shifts, eliminate(groups, lambda k: half + k, LEAF_PANEL)):
+    for shift, (left, right) in zip(shifts, eliminate(groups, lambda k: half + k, panel)):
         inverse = jnp.concatenate(right, axis=0)
         upper = jnp.where(col >= row, jnp.concatenate(left, axis=0), 0.0)
         out.append((inverse, jnp.where(row < rank, upper - shift * inverse, 0.0)))
@@ -331,6 +331,20 @@
     return lax.dot_general(
         a, b, (((1,), (1,)), ((), ())), precision=HIGH, preferred_element_type=F32
     )
+
+
+def wide(gram):
+    return jnp.concatenate([gram[: S // 2], gram[S // 2 :]], axis=1)
+
+
+def square_of(value):
+    return jnp.concatenate([value[:, :S], value[:, S:]], axis=0)
+
+
+def send_all(gram, ref):
+    value = wide(gram)
+    for k in range(ref.shape[0]):
+        ref[k] = value
 
 
 def keep_first(value, rank):
@@ -367,8 +381,10 @@
         grams = []
         for p in range(LEAF_PAIRS):
             pair = jnp.concatenate([sample_ref[first + 2 * p + k] for k in range(2)], axis=0)
-            grams.append(times_t(pair, pair))
-        for p, (inverse, projected) in enumerate(factor_pairs(grams, rank_ref[0])):
+            both = times_t(pair, pair)
+            first_box = lax.broadcasted_iota(jnp.int32, (S, 2 * S), 1) < S
+            grams.append(jnp.where(first_box, both[:S], both[S:]))
+        for p, (inverse, projected) in enumerate(factor_pairs(grams, rank_ref[0], LEAF_PANEL)):
             for k in range(2):
                 inv_ref[first + 2 * p + k] = inverse[:, k * S : k * S + S]
                 proj_ref[first + 2 * p + k] = projected[:, k * S : k * S + S]
@@ -379,7 +395,7 @@
     inverse, current, _ = factor_one(gram, rank_ref[1])
     inv1_ref[...] = inverse
     cur_ref[...] = current
-    gram_ref[...] = gram_of(current)
+    send_all(gram_of(current), gram_ref)
 
 
 def smem_spec():
@@ -395,7 +411,7 @@
     many = vmem((8, S, S), F32)
     return pl.pallas_call(
         halo_y_body,
-        out_shape=(vmem((8, S, N), F32), many, many, small, small, small),
+        out_shape=(vmem((8, S, N), F32), many, many, small, small, vmem((16, S // 2, 2 * S), F32)),
         in_specs=[smem_spec()] + [vmem_spec()] * 4,
         scratch_shapes=[
             vmem((16, N, FEAT), BF16),
@@ -410,50 +426,75 @@
     return keep_first(times_t(inverse, current), rank) * math.sqrt(S)
 
 
-def upper_body(height, rank_ref, g0, g1, g2, g3, *refs):
-    gram = (g0[...] + g1[...]) + (g2[...] + g3[...])
-    rank = rank_ref[height]
-    if height == 2:
-        inv1_in, proj_in, inv_ref, cur_ref, gram_ref, leaf_ref = refs
-        for b in range(8):
-            leaf_ref[b] = transfer_of(inv1_in[...], proj_in[b], rank_ref[1])
-    elif height == 3:
-        inv_in, cur_in, leaf_in, sample_in, inv_ref, cur_ref, gram_ref, done_ref, basis_ref = refs
-        done_ref[...] = transfer_of(inv_in[...], cur_in[...], rank_ref[2])
-        for b in range(8):
-            basis = jnp.dot(leaf_in[b], sample_in[b], precision=HIGH, preferred_element_type=F32)
-            basis_ref[b] = (keep_first(basis, rank_ref[0]) * math.sqrt(N)).astype(BF16)
-    else:
-        inv_in, cur2_in, cur_in, done_in, upper_ref, top_ref = refs
-        upper_ref[0] = done_in[...]
-        upper_ref[1] = transfer_of(inv_in[...], cur2_in[...], rank_ref[3])
-    inverse, current, trace = factor_one(gram, rank)
-    if height == 4:
-        upper_ref[2] = transfer_of(inverse, cur_in[...], rank)
-        top_ref[...] = current / jnp.sqrt(trace / S + TINY)
-        return
-    inv_ref[...] = inverse
-    cur_ref[...] = current
-    gram_ref[...] = gram_of(current)
-
-
-def upper(height, ranks, grams, extra):
+def transfer_of(inverse, current, rank):
+    return keep_first(times_t(inverse, current), rank) * math.sqrt(S)
+
+
+def upper23_body(
+    rank_ref, gram_in, inv1_in, proj_in, cur1_in, leaf_in, sample_in,
+    leaf_ref, basis_ref, done_ref, inv3_ref, own2_ref, cur3_ref, gram_ref, inv2_ref, cur2_ref,
+):
+    for b in range(8):
+        leaf_ref[b] = transfer_of(inv1_in[...], proj_in[b], rank_ref[1])
+        basis = jnp.dot(leaf_in[b], sample_in[b], precision=HIGH, preferred_element_type=F32)
+        basis_ref[b] = (keep_first(basis, rank_ref[0]) * math.sqrt(N)).astype(BF16)
+    sums = []
+    for qa in range(2):
+        for qb in range(2):
+            corner = qa * 8 + qb * 2
+            sums.append(
+                (gram_in[corner] + gram_in[corner + 1]) + (gram_in[corner + 4] + gram_in[corner + 5])
+            )
+    grams = [
+        jnp.concatenate([square_of(sums[2 * p]), square_of(sums[2 * p + 1])], axis=1)
+        for p in range(2)
+    ]
+    for p, (inverse, current) in enumerate(factor_pairs(grams, rank_ref[2], PAIR_PANEL)):
+        for k in range(2):
+            inv2_ref[2 * p + k] = inverse[:, k * S : k * S + S]
+            cur2_ref[2 * p + k] = current[:, k * S : k * S + S]
+    gram = gram_of(cur2_ref[...].reshape(4 * S, S))
+    own = ((lax.axis_index("leaf") >> 1) & 1) * 2 + ((lax.axis_index("brick") >> 1) & 1)
+    done_ref[...] = transfer_of(inv2_ref[own], cur1_in[...], rank_ref[2])
+    own2_ref[...] = cur2_ref[own]
+    inverse, current, _ = factor_one(gram, rank_ref[3])
+    inv3_ref[...] = inverse
+    cur3_ref[...] = current
+    send_all(gram_of(current), gram_ref)
+
+
+def upper23(ranks, *values):
     small = vmem((S, S), F32)
-    out = {
-        2: (small,) * 3 + (jax.ShapeDtypeStruct((8, S, S), F32),),
-        3: (small,) * 4 + (jax.ShapeDtypeStruct((8, S, N), BF16),),
-        4: (jax.ShapeDtypeStruct((3, S, S), F32), jax.ShapeDtypeStruct((S, S), F32)),
-    }[height]
-
-    def body(*refs):
-        upper_body(height, *refs)
-
     return pl.pallas_call(
-        body,
-        out_shape=out,
-        in_specs=[smem_spec()] + [vmem_spec()] * (4 + len(extra)),
-        name="upper" + str(height),
-    )(ranks, *(near(value) for value in (*grams, *extra)))
+        upper23_body,
+        out_shape=(
+            jax.ShapeDtypeStruct((8, S, S), F32),
+            jax.ShapeDtypeStruct((8, S, N), BF16),
+            small, small, small, small,
+            vmem((4, S // 2, 2 * S), F32),
+        ),
+        in_specs=[smem_spec()] + [vmem_spec()] * len(values),
+        scratch_shapes=[vmem((4, S, S), F32), vmem((4, S, S), F32)],
+        name="upper23",
+    )(ranks, *(near(value) for value in values))
+
+
+def upper4_body(rank_ref, gram_in, inv3_in, cur2_in, cur3_in, done_in, upper_ref, top_ref):
+    upper_ref[0] = done_in[...]
+    upper_ref[1] = transfer_of(inv3_in[...], cur2_in[...], rank_ref[3])
+    gram = square_of((gram_in[0] + gram_in[1]) + (gram_in[2] + gram_in[3]))
+    inverse, current, trace = factor_one(gram, rank_ref[4])
+    upper_ref[2] = transfer_of(inverse, cur3_in[...], rank_ref[4])
+    top_ref[...] = current / jnp.sqrt(trace / S + TINY)
+
+
+def upper4(ranks, *values):
+    return pl.pallas_call(
+        upper4_body,
+        out_shape=(jax.ShapeDtypeStruct((3, S, S), F32), jax.ShapeDtypeStruct((S, S), F32)),
+        in_specs=[smem_spec()] + [vmem_spec()] * len(values),
+        name="upper4",
+    )(ranks, *(near(value) for value in values))
 
 
 def shift_pair(head, tail, axis):
@@ -463,15 +504,22 @@
     return lax.ppermute(tail, axis, up), lax.ppermute(head, axis, down)
 
 
-def siblings(value, flip_leaf, flip_brick):
+def spread_bits(bits):
+    out = [0]
+    for bit in bits:
+        out = out + [value | 1 << bit for value in out]
+    return out
+
+
+def gather_siblings(copies, bits):
     rows, cols = lax.axis_size("leaf"), lax.axis_size("brick")
-    out = [value]
-    for dx, dy in ((0, flip_brick), (flip_leaf, 0), (flip_leaf, flip_brick)):
-        perm = [
-            (i * cols + j, (i ^ dx) * cols + (j ^ dy)) for i in range(rows) for j in range(cols)
-        ]
-        out.append(lax.ppermute(value, ("leaf", "brick"), perm))
-    return out
+    flips = spread_bits(bits)
+    groups = [
+        [(i | a) * cols + (j | b) for a in flips for b in flips]
+        for i in range(rows) if not i & flips[-1]
+        for j in range(cols) if not j & flips[-1]
+    ]
+    return lax.all_to_all(copies, ("leaf", "brick"), 0, 0, axis_index_groups=groups, tiled=True)
 
 
 def shards(points, test_matrix, trunc_ranks):
@@ -490,14 +538,11 @@
     sample, inverse, projected, inverse1, current1, gram = halo_y(
         trunc_ranks, own_points, below.reshape(8, rows, N), above.reshape(8, rows, N), part
     )
-    inverse2, current2, gram, transfer = upper(
-        2, trunc_ranks, siblings(gram, 1, 1), (inverse1, projected)
-    )
-    inverse3, current3, gram, done2, basis = upper(
-        3, trunc_ranks, siblings(gram, 3, 2), (inverse2, current1, inverse, sample)
-    )
-    uppers, top = upper(
-        4, trunc_ranks, siblings(gram, 4, 4), (inverse3, current2, current3, done2)
+    transfer, basis, done2, inverse3, current2, current3, gram = upper23(
+        trunc_ranks, gather_siblings(gram, (0, 1)), inverse1, projected, current1, inverse, sample
+    )
+    uppers, top = upper4(
+        trunc_ranks, gather_siblings(gram, (2,)), inverse3, current2, current3, done2
     )
     block = points.shape[:3]
     return (

time: 89.6 us -> 76.4 us (0.85)
  starting transfers between devices: 45.2 us -> 8.44 us
  blocking collectives: 0 us -> 32.6 us
  waiting for transfers between devices: 10.3 us -> 1.44 us
    ppermute x9 -> x0, starting transfers between devices: 36.8 us -> none  [siblings(): out.append(lax.ppermute(value, ('leaf', 'brick'), perm))]
    all_to_all x0 -> x2, blocking collectives: none -> 32.6 us  [gather_siblings(): lax.all_to_all(copies, ('leaf', 'brick'), 0, 0, axis_index_groups=groups,...]
    ppermute x9 -> x0, waiting for transfers between devices: 8.87 us -> none  [siblings(): out.append(lax.ppermute(value, ('leaf', 'brick'), perm))]
    pallas_call x3 -> x2, Pallas kernels: 8.51 us -> 8.65 us  [the longest x1 5.72 us: upper23(): pl.pallas_call(upper23_body, out_shape=(jax.ShapeDtypeStruct((8, S, S), F...]
  transfers between devices with their start and end apart: 13 -> 4, of which waited for: 6 -> 1; matrix products, arithmetic and copies ran while one was open for 0% -> 0% of each run, Pallas kernels for 12% -> 14%
where the time goes in v2:
time: 76.4 us; the launch traced here: 75.8 us
  blocking collectives  32.6 us (43%)
  Pallas kernels  30.8 us (40%)
  starting transfers between devices  8.44 us (11%)
  local copies, waits for them, and re-layouts  1.66 us (2%)
  waiting for transfers between devices  1.44 us (2%)
    all_to_all x2, blocking collectives, gather_siblings(): lax.all_to_all(copies, ('leaf', 'brick'), 0, 0, axis_index_groups=groups,...  32.6 us
    pallas_call x1, Pallas kernels, halo_y(): pl.pallas_call(halo_y_body, out_shape=(vmem((8, S, N), F32), many, many,...  11.6 us
    ppermute x4, starting transfers between devices, shift_pair(): return (lax.ppermute(tail, axis, up), lax.ppermute(head, axis, down))  8.44 us
    pallas_call x1, Pallas kernels, own_pairs(): pl.pallas_call(own_pairs_body, out_shape=vmem((8, S, N), F32), scratch_sh...  5.74 us
    pallas_call x1, Pallas kernels, upper23(): pl.pallas_call(upper23_body, out_shape=(jax.ShapeDtypeStruct((8, S, S), F...  5.72 us
    pallas_call x1, Pallas kernels, halo_x(): pl.pallas_call(halo_x_body, out_shape=vmem((8, S, N), F32), in_specs=[vme...  4.87 us
    pallas_call x1, Pallas kernels, upper4(): pl.pallas_call(upper4_body, out_shape=(jax.ShapeDtypeStruct((3, S, S), F3...  2.93 us
  transfers between devices with their start and end apart: 4, of which 1 were waited for; matrix products, arithmetic and copies ran while one was open for 0% of the time, Pallas kernels for 14%

profile of v2, /device:TPU:128, one launch (start us, length us, event | category | flops | bytes accessed | tf_op | source)
XLA Modules:
  0.0 75.8 jit_solution(11755919236286628595)
XLA Ops:
  0.6 0.0 copy-start
  0.6 1.0 %constant_dynamic-update-slice_fusion.1 = bf16[2,2,2,67,256]{4,3,2,1,0:T(8,128)(2,1)S(1)} fusion(bf16[2,2,2,64,256]{4,3,2,1,0:T(8,128)(2,1)} %param.4), kind=kLoop, calls=%fused_computation.3 | loop fusion | bytes 524288
  1.6 0.0 copy-done
  1.6 0.6 constant_dynamic-update-slice_fusion
  2.3 3.8 %collective-permute-start.1 = (bf16[1,2,2,67,256]{4,3,2,1,0:T(8,128)(2,1)S(1)}, bf16[1,2,2,67,256]{4,3,2,1,0:T(8,128)(2,1)S(1)}, u32[]{:S(2)}, u32[]{:S(2)}) collective-permute-start(bf16[1,2,2,67,256]{4,3,2,1,0:T(8,128)(2,1)S(1)} %get-tuple-element.46), channel_id=1, source_target_pairs={{16,0},{32,16},{48,32},{64,48},{80,64},{96,80},{112,96},{128,112},... | collective-permute-start | bytes 411656 | tf_op jit(solution)/shard_map/ppermute | solution.py:504
  6.0 2.1 %collective-permute-start = (bf16[1,2,2,67,256]{4,3,2,1,0:T(8,128)(2,1)S(1)}, bf16[1,2,2,67,256]{4,3,2,1,0:T(8,128)(2,1)S(1)}, u32[]{:S(2)}, u32[]{:S(2)}) collective-permute-start(bf16[1,2,2,67,256]{4,3,2,1,0:T(8,128)(2,1)S(1)} %get-tuple-element.47), channel_id=1, source_target_pairs={{0,16},{16,32},{32,48},{48,64},{64,80},{80,96},{96,112},{112,128},... | collective-permute-start | bytes 411656 | tf_op jit(solution)/shard_map/ppermute | solution.py:504
  8.1 5.7 %own_pairs.1.part_ref = f32[8,64,256]{2,1,0:T(8,128)S(1)} custom-call(bf16[8,3,256]{2,1,0:T(4,128)(2,1)} %bitcast.17, bf16[8,64,256]{2,1,0:T(8,128)(2,1)} %bitcast.16), custom_call_target="tpu_custom_call" | custom-call | tf_op jit(solution)/shard_map/own_pairs/pallas_call | solution.py:149
  13.9 0.0 collective-permute-done.1
  13.9 1.4 %collective-permute-done = bf16[1,2,2,67,256]{4,3,2,1,0:T(8,128)(2,1)S(1)} collective-permute-done((bf16[1,2,2,67,256]{4,3,2,1,0:T(8,128)(2,1)S(1)}, bf16[1,2,2,67,256]{4,3,2,1,0:T(8,128)(2,1)S(1)}, u32[]{:S(2)}, u32[]{:S(2)}) %collective-permute-start) | collective-permute-done | bytes 137248 | tf_op jit(solution)/shard_map/ppermute | solution.py:504
  15.4 1.3 %collective-permute-start.2 = (bf16[4,1,2,67,256]{4,3,2,1,0:T(8,128)(2,1)S(1)}, bf16[4,1,2,67,256]{4,3,2,1,0:T(8,128)(2,1)S(1)}, u32[]{:S(2)}, u32[]{:S(2)}) collective-permute-start(bf16[4,1,2,67,256]{4,3,2,1,0:T(8,128)(2,1)S(1)} %pad_maximum_fusion), channel_id=1, source_target_pairs={{0,1},{1,2},{2,3},{3,4},{4,5},{5,6},{6,7},{7,8},{8,9},{9,10},{10,1... | collective-permute-start | bytes 823304 | tf_op jit(solution)/shard_map/ppermute | solution.py:504
  16.8 1.3 %collective-permute-start.3 = (bf16[4,1,2,67,256]{4,3,2,1,0:T(8,128)(2,1)S(1)}, bf16[4,1,2,67,256]{4,3,2,1,0:T(8,128)(2,1)S(1)}, u32[]{:S(2)}, u32[]{:S(2)}) collective-permute-start(bf16[4,1,2,67,256]{4,3,2,1,0:T(8,128)(2,1)S(1)} %pad_maximum_fusion.1), channel_id=1, source_target_pairs={{1,0},{2,1},{3,2},{4,3},{5,4},{6,5},{7,6},{8,7},{9,8},{10,9},{11,1... | collective-permute-start | bytes 823304 | tf_op jit(solution)/shard_map/ppermute | solution.py:504
  18.1 4.9 %halo_x.1.part_ref = f32[8,64,256]{2,1,0:T(8,128)S(1)} custom-call(bf16[8,3,256]{2,1,0:T(4,128)(2,1)} %bitcast.18, bf16[4,67,256]{2,1,0:T(8,128)(2,1)S(1)} %bitcast.13, bf16[4,67,256]{2,1,0:T(8,128)(2,1)S(1)} %bitcast.12, f32[8,64,256]{2,1,0:T(8,128)S(1)} %own_pairs.1.part_ref), custom_call_target="tpu_custom_call" | custom-call | tf_op jit(solution)/shard_map/halo_x/pallas_call | solution.py:207
  23.0 0.0 collective-permute-done.2
  23.0 0.0 collective-permute-done.3
  23.0 11.6 %halo_y.1 = (f32[8,64,256]{2,1,0:T(8,128)S(1)}, f32[8,64,64]{2,1,0:T(8,128)S(1)}, f32[8,64,64]{2,1,0:T(8,128)S(1)}, f32[64,64]{1,0:T(8,128)S(1)}, f32[64,64]{1,0:T(8,128)S(1)}, /*index=5*/f32[16,32,128]{2,1,0:T(8,128)S(1)}) custom-call(s32[5]{0:T(128)} %rank_ref.5, bf16[8,3,256]{2,1,0:T(4,128)(2,1)} %bitcast.19, bf16[8,67,256]{2,1,0:T(8,128)(2,1)S(1)} %bitcast.14, ...), custom_call_target="tpu_custom_call" | custom-call | tf_op jit(solution)/shard_map/halo_y/pallas_call | solution.py:412
  34.5 17.4 %all_to_all.10.gram_in = f32[16,32,128]{2,1,0:T(8,128)S(1)} all-to-all(f32[16,32,128]{2,1,0:T(8,128)S(1)} %get-tuple-element.25), channel_id=1, replica_groups={{0,1,2,3,16,17,18,19,32,33,34,35,48,49,50,51},{4,5,6,7,20,21,22,23,36,3..., dimensions={0} | all-to-all | bytes 524288 | tf_op jit(solution)/shard_map/all_to_all | solution.py:522
  52.0 5.7 %upper23.1 = (f32[8,64,64]{2,1,0:T(8,128)}, bf16[8,64,256]{2,1,0:T(8,128)(2,1)}, f32[64,64]{1,0:T(8,128)S(1)}, f32[64,64]{1,0:T(8,128)S(1)}, f32[64,64]{1,0:T(8,...) custom-call(s32[5]{0:T(128)} %rank_ref.5, f32[16,32,128]{2,1,0:T(8,128)S(1)} %all_to_all.10.gram_in, ...), custom_call_target="tpu_custom_call" | custom-call | tf_op jit(solution)/shard_map/upper23/pallas_call | solution.py:468
  57.7 15.2 %all_to_all.11.gram_in = f32[4,32,128]{2,1,0:T(8,128)S(1)} all-to-all(f32[4,32,128]{2,1,0:T(8,128)S(1)} %get-tuple-element.33), channel_id=1, replica_groups={{0,4,64,68},{1,5,65,69},{2,6,66,70},{3,7,67,71},{8,12,72,76},{9,13,73,7..., dimensions={0} | all-to-all | bytes 131072 | tf_op jit(solution)/shard_map/all_to_all | solution.py:522
  72.9 2.9 %upper4.1 = (f32[3,64,64]{2,1,0:T(8,128)}, f32[64,64]{1,0:T(8,128)}) custom-call(s32[5]{0:T(128)} %rank_ref.5, f32[4,32,128]{2,1,0:T(8,128)S(1)} %all_to_all.11.gram_in, f32[64,64]{1,0:T(8,128)S(1)} %get-tuple-element.34.inv3_in, f32[64,64]{1,0:T(8,128)S(1)} %get-tuple-element.35.cur2_in, f32[64,64]{1,0:T(8,128)S(1)} %get-tuple-element.36.cur3_in, ...), custom_call_target="tpu_custom_call" | custom-call | tf_op jit(solution)/shard_map/upper4/pallas_call | solution.py:492
  (5 shorter events, 0.1 us)
Async XLA Ops:
  0.6 1.0 %copy-start = (bf16[2,2,2,3,256]{4,2,3,1,0:T(2,128)(2,1)S(1)}, bf16[2,2,2,3,256]{4,2,3,1,0:T(2,128)(2,1)}, u32[]{:S(2)}) copy-start(bf16[2,2,2,3,256]{4,2,3,1,0:T(2,128)(2,1)} %param.3) | copy-start | bytes 36868
  2.3 11.6 %collective-permute-start.1 = (bf16[1,2,2,67,256]{4,3,2,1,0:T(8,128)(2,1)S(1)}, bf16[1,2,2,67,256]{4,3,2,1,0:T(8,128)(2,1)S(1)}, u32[]{:S(2)}, u32[]{:S(2)}) collective-permute-start(bf16[1,2,2,67,256]{4,3,2,1,0:T(8,128)(2,1)S(1)} %get-tuple-element.46), channel_id=1, source_target_pairs={{16,0},{32,16},{48,32},{64,48},{80,64},{96,80},{112,96},{128,112},... | collective-permute-start | bytes 411656 | tf_op jit(solution)/shard_map/ppermute | solution.py:504
  6.0 9.3 %collective-permute-start = (bf16[1,2,2,67,256]{4,3,2,1,0:T(8,128)(2,1)S(1)}, bf16[1,2,2,67,256]{4,3,2,1,0:T(8,128)(2,1)S(1)}, u32[]{:S(2)}, u32[]{:S(2)}) collective-permute-start(bf16[1,2,2,67,256]{4,3,2,1,0:T(8,128)(2,1)S(1)} %get-tuple-element.47), channel_id=1, source_target_pairs={{0,16},{16,32},{32,48},{48,64},{64,80},{80,96},{96,112},{112,128},... | collective-permute-start | bytes 411656 | tf_op jit(solution)/shard_map/ppermute | solution.py:504
  15.4 7.5 %collective-permute-start.2 = (bf16[4,1,2,67,256]{4,3,2,1,0:T(8,128)(2,1)S(1)}, bf16[4,1,2,67,256]{4,3,2,1,0:T(8,128)(2,1)S(1)}, u32[]{:S(2)}, u32[]{:S(2)}) collective-permute-start(bf16[4,1,2,67,256]{4,3,2,1,0:T(8,128)(2,1)S(1)} %pad_maximum_fusion), channel_id=1, source_target_pairs={{0,1},{1,2},{2,3},{3,4},{4,5},{5,6},{6,7},{7,8},{8,9},{9,10},{10,1... | collective-permute-start | bytes 823304 | tf_op jit(solution)/shard_map/ppermute | solution.py:504
  16.8 6.2 %collective-permute-start.3 = (bf16[4,1,2,67,256]{4,3,2,1,0:T(8,128)(2,1)S(1)}, bf16[4,1,2,67,256]{4,3,2,1,0:T(8,128)(2,1)S(1)}, u32[]{:S(2)}, u32[]{:S(2)}) collective-permute-start(bf16[4,1,2,67,256]{4,3,2,1,0:T(8,128)(2,1)S(1)} %pad_maximum_fusion.1), channel_id=1, source_target_pairs={{1,0},{2,1},{3,2},{4,3},{5,4},{6,5},{7,6},{8,7},{9,8},{10,9},{11,1... | collective-permute-start | bytes 823304 | tf_op jit(solution)/shard_map/ppermute | solution.py:504

commit v3 on v2

--- a/solution.py
+++ b/solution.py
@@ -158,6 +158,40 @@
     )(points, tests)
 
 
+def pack_body(pts_ref, tst_ref, head_ref, tail_ref, south_ref, north_ref):
+    for x, x_face in enumerate((head_ref, tail_ref)):
+        for y, y_face in enumerate((south_ref, north_ref)):
+            for z in range(2):
+                box = x * 4 + y * 2 + z
+                for face, slot in ((x_face, y * 2 + z), (y_face, x * 2 + z)):
+                    face[slot, :S, :] = tst_ref[box]
+                    face[slot, S : S + 3, :] = pts_ref[box]
+
+
+def pack(points, tests):
+    return pl.pallas_call(
+        pack_body, out_shape=(vmem((4, S + 3, N), BF16),) * 4, name="pack"
+    )(points, tests)
+
+
+def edges_body(low_ref, high_ref, south_in, north_in, south_ref, north_ref):
+    for y, (mid, out) in enumerate(((south_in, south_ref), (north_in, north_ref))):
+        for z in range(2):
+            out[z] = low_ref[y * 2 + z]
+            out[6 + z] = high_ref[y * 2 + z]
+        for slot in range(4):
+            out[2 + slot] = mid[slot]
+
+
+def edges(*values):
+    return pl.pallas_call(
+        edges_body,
+        out_shape=(vmem((8, S + 3, N), BF16),) * 2,
+        in_specs=[vmem_spec()] * len(values),
+        name="edges",
+    )(*(near(value) for value in values))
+
+
 def halo_tiles(jobs, own, part_ref, out_ref, left_ref, halo_ref, base_ref, slope_ref):
     totals = [part_ref[own + bz] for bz in range(2)]
 
@@ -176,18 +210,18 @@
         out_ref[own + bz] = totals[bz]
 
 
-def halo_prep(pts_ref, sides, left_ref, base_ref, slope_ref):
+def halo_prep(sides, left_ref):
     count = sides[0].shape[0]
     for side, ref in enumerate(sides):
         for box in range(count):
             put_left(ref[box, S : S + 3, :], left_ref, side * count + box)
+
+
+def halo_x_body(pts_ref, low_ref, high_ref, part_ref, out_ref, left_ref, base_ref, slope_ref):
+    sides = (low_ref, high_ref)
+    halo_prep(sides, left_ref)
     for b in range(8):
         put_right(pts_ref[b], base_ref, slope_ref, b)
-
-
-def halo_x_body(pts_ref, low_ref, high_ref, part_ref, out_ref, left_ref, base_ref, slope_ref):
-    sides = (low_ref, high_ref)
-    halo_prep(pts_ref, sides, left_ref, base_ref, slope_ref)
     for i, side in enumerate(sides):
 
         def step(j, carry):
@@ -203,18 +237,18 @@
         lax.fori_loop(0, 2, step, 0)
 
 
-def halo_x(points, low, high, part):
+def halo_x(points, *values):
     return pl.pallas_call(
         halo_x_body,
         out_shape=vmem((8, S, N), F32),
-        in_specs=[vmem_spec()] * 4,
+        in_specs=[vmem_spec()] * (1 + len(values)),
         scratch_shapes=[
             vmem((8, N, FEAT), BF16),
             vmem((8, FEAT, N), F32),
             vmem((8, FEAT, N), F32),
         ],
         name="halo_x",
-    )(points, near(low), near(high), near(part))
+    )(points, *(near(value) for value in values))
 
 
 def spread_row(block, row):
@@ -358,7 +392,9 @@
     left_ref, base_ref, slope_ref,
 ):
     sides = (low_ref, high_ref)
-    halo_prep(pts_ref, sides, left_ref, base_ref, slope_ref)
+    halo_prep(sides, left_ref)
+    for b in range(8):
+        put_right(pts_ref[b], base_ref, slope_ref, b)
     for j, side in enumerate(sides):
 
         def step(i, carry):
@@ -406,20 +442,20 @@
     return pl.BlockSpec(memory_space=pltpu.VMEM)
 
 
-def halo_y(ranks, points, low, high, part):
+def halo_y(ranks, points, *values):
     small = vmem((S, S), F32)
     many = vmem((8, S, S), F32)
     return pl.pallas_call(
         halo_y_body,
         out_shape=(vmem((8, S, N), F32), many, many, small, small, vmem((16, S // 2, 2 * S), F32)),
-        in_specs=[smem_spec()] + [vmem_spec()] * 4,
+        in_specs=[smem_spec()] + [vmem_spec()] * (1 + len(values)),
         scratch_shapes=[
             vmem((16, N, FEAT), BF16),
             vmem((8, FEAT, N), F32),
             vmem((8, FEAT, N), F32),
         ],
         name="halo_y",
-    )(ranks, points, near(low), near(high), near(part))
+    )(ranks, points, *(near(value) for value in values))
 
 
 def transfer_of(inverse, current, rank):
@@ -523,20 +559,17 @@
 
 
 def shards(points, test_matrix, trunc_ranks):
-    packed = jnp.concatenate([test_matrix, points], axis=3)
-    rows = S + 3
     own_points = points.reshape(8, 3, N)
     own_tests = test_matrix.reshape(8, S, N)
-    low, high = shift_pair(packed[:1], packed[1:], "leaf")
+    head, tail, south, north = pack(own_points, own_tests)
+    low, high = shift_pair(head, tail, "leaf")
     part = own_pairs(own_points, own_tests)
     low, high, part = lax.optimization_barrier((low, high, part))
-    wide = [low, packed, high]
-    south = jnp.concatenate([w[:, :1] for w in wide], axis=0)
-    north = jnp.concatenate([w[:, 1:] for w in wide], axis=0)
+    south, north = edges(low, high, south, north)
     below, above = shift_pair(south, north, "brick")
-    part = halo_x(own_points, low.reshape(4, rows, N), high.reshape(4, rows, N), part)
+    part = halo_x(own_points, low, high, part)
     sample, inverse, projected, inverse1, current1, gram = halo_y(
-        trunc_ranks, own_points, below.reshape(8, rows, N), above.reshape(8, rows, N), part
+        trunc_ranks, own_points, below, above, part
     )
     transfer, basis, done2, inverse3, current2, current3, gram = upper23(
         trunc_ranks, gather_siblings(gram, (0, 1)), inverse1, projected, current1, inverse, sample

time: 76.4 us -> 78.1 us (1.022)
  starting transfers between devices: 8.44 us -> 10.6 us
  waiting for transfers between devices: 1.44 us -> 0.01 us
  Pallas kernels: 30.8 us -> 31.9 us
    ppermute x4, starting transfers between devices: 8.44 us -> 10.6 us  [shift_pair(): return (lax.ppermute(tail, axis, up), lax.ppermute(head, axis, down))]
    ppermute x4, waiting for transfers between devices: 1.44 us -> 0.01 us  [shift_pair(): return (lax.ppermute(tail, axis, up), lax.ppermute(head, axis, down))]
    pallas_call x0 -> x2, Pallas kernels: none -> 1.05 us  [the longest x1 1.01 us: pack(): pl.pallas_call(pack_body, out_shape=(vmem((4, S + 3, N), BF16),) * 4, nam...]
  transfers between devices with their start and end apart: 4 -> 4, of which waited for: 1 -> 0; matrix products, arithmetic and copies ran while one was open for 0% -> 0% of each run, Pallas kernels for 14% -> 14%
where the time goes in v3:
time: 78.1 us; the launch traced here: 77.4 us
  blocking collectives  32.9 us (42%)
  Pallas kernels  31.9 us (41%)
  starting transfers between devices  10.6 us (14%)
  local copies, waits for them, and re-layouts  1.32 us (2%)
    all_to_all x2, blocking collectives, gather_siblings(): lax.all_to_all(copies, ('leaf', 'brick'), 0, 0, axis_index_groups=groups,...  32.9 us
    pallas_call x1, Pallas kernels, halo_y(): pl.pallas_call(halo_y_body, out_shape=(vmem((8, S, N), F32), many, many,...  11.6 us
    ppermute x4, starting transfers between devices, shift_pair(): return (lax.ppermute(tail, axis, up), lax.ppermute(head, axis, down))  10.6 us
    pallas_call x1, Pallas kernels, own_pairs(): pl.pallas_call(own_pairs_body, out_shape=vmem((8, S, N), F32), scratch_sh...  5.74 us
    pallas_call x1, Pallas kernels, upper23(): pl.pallas_call(upper23_body, out_shape=(jax.ShapeDtypeStruct((8, S, S), F...  5.72 us
    pallas_call x1, Pallas kernels, halo_x(): pl.pallas_call(halo_x_body, out_shape=vmem((8, S, N), F32), in_specs=[vme...  4.87 us
    pallas_call x1, Pallas kernels, upper4(): pl.pallas_call(upper4_body, out_shape=(jax.ShapeDtypeStruct((3, S, S), F3...  2.93 us
  transfers between devices with their start and end apart: 4, of which 0 were waited for; matrix products, arithmetic and copies ran while one was open for 0% of the time, Pallas kernels for 14%

profile of v3, /device:TPU:128, one launch (start us, length us, event | category | flops | bytes accessed | tf_op | source)
XLA Modules:
  0.0 77.4 jit_solution(7124694842340334972)
XLA Ops:
  0.6 1.3 %copy.7 = bf16[2,2,2,3,256]{4,3,2,1,0:T(4,128)(2,1)} copy(bf16[2,2,2,3,256]{4,2,3,1,0:T(2,128)(2,1)} %param.3) | data formatting | bytes 24576 | tf_op args[0]
  2.0 1.0 %pack.1 = (bf16[4,67,256]{2,1,0:T(8,128)(2,1)S(1)}, bf16[4,67,256]{2,1,0:T(8,128)(2,1)S(1)}, bf16[4,67,256]{2,1,0:T(8,128)(2,1)S(1)}, bf16[4,67,256]{2,1,0:T(8,128)(2,1)S(1)}) custom-call(bf16[8,3,256]{2,1,0:T(4,128)(2,1)} %bitcast.10, bf16[8,64,256]{2,1,0:T(8,128)(2,1)} %bitcast.8), custom_call_target="tpu_custom_call" | custom-call | tf_op jit(solution)/shard_map/pack/pallas_call | solution.py:172
  3.0 3.4 %collective-permute-start = (bf16[4,67,256]{2,1,0:T(8,128)(2,1)S(1)}, bf16[4,67,256]{2,1,0:T(8,128)(2,1)S(1)}, u32[]{:S(2)}, u32[]{:S(2)}) collective-permute-start(bf16[4,67,256]{2,1,0:T(8,128)(2,1)S(1)} %get-tuple-element.28), channel_id=1, source_target_pairs={{0,16},{16,32},{32,48},{48,64},{64,80},{80,96},{96,112},{112,128},... | collective-permute-start | bytes 411656 | tf_op jit(solution)/shard_map/ppermute | solution.py:540
  6.4 4.6 %collective-permute-start.1 = (bf16[4,67,256]{2,1,0:T(8,128)(2,1)S(1)}, bf16[4,67,256]{2,1,0:T(8,128)(2,1)S(1)}, u32[]{:S(2)}, u32[]{:S(2)}) collective-permute-start(bf16[4,67,256]{2,1,0:T(8,128)(2,1)S(1)} %get-tuple-element.29), channel_id=1, source_target_pairs={{16,0},{32,16},{48,32},{64,48},{80,64},{96,80},{112,96},{128,112},... | collective-permute-start | bytes 411656 | tf_op jit(solution)/shard_map/ppermute | solution.py:540
  10.9 5.7 %own_pairs.1.part_ref = f32[8,64,256]{2,1,0:T(8,128)S(1)} custom-call(bf16[8,3,256]{2,1,0:T(4,128)(2,1)} %bitcast.11, bf16[8,64,256]{2,1,0:T(8,128)(2,1)} %bitcast.9), custom_call_target="tpu_custom_call" | custom-call | tf_op jit(solution)/shard_map/own_pairs/pallas_call | solution.py:149
  16.7 0.0 collective-permute-done.low_ref
  16.7 0.0 collective-permute-done.1.high_ref
  16.8 1.3 %collective-permute-start.2 = (bf16[8,67,256]{2,1,0:T(8,128)(2,1)S(1)}, bf16[8,67,256]{2,1,0:T(8,128)(2,1)S(1)}, u32[]{:S(2)}, u32[]{:S(2)}) collective-permute-start(bf16[8,67,256]{2,1,0:T(8,128)(2,1)S(1)} %get-tuple-element.34), channel_id=1, source_target_pairs={{0,1},{1,2},{2,3},{3,4},{4,5},{5,6},{6,7},{7,8},{8,9},{9,10},{10,1... | collective-permute-start | bytes 823304 | tf_op jit(solution)/shard_map/ppermute | solution.py:540
  18.1 1.3 %collective-permute-start.3 = (bf16[8,67,256]{2,1,0:T(8,128)(2,1)S(1)}, bf16[8,67,256]{2,1,0:T(8,128)(2,1)S(1)}, u32[]{:S(2)}, u32[]{:S(2)}) collective-permute-start(bf16[8,67,256]{2,1,0:T(8,128)(2,1)S(1)} %get-tuple-element.35), channel_id=1, source_target_pairs={{1,0},{2,1},{3,2},{4,3},{5,4},{6,5},{7,6},{8,7},{9,8},{10,9},{11,1... | collective-permute-start | bytes 823304 | tf_op jit(solution)/shard_map/ppermute | solution.py:540
  19.4 4.9 %halo_x.1.part_ref = f32[8,64,256]{2,1,0:T(8,128)S(1)} custom-call(bf16[8,3,256]{2,1,0:T(4,128)(2,1)} %bitcast.12, bf16[4,67,256]{2,1,0:T(8,128)(2,1)S(1)} %collective-permute-done.low_ref, bf16[4,67,256]{2,1,0:T(8,128)(2,1)S(1)} %collective-permute-done.1.high_ref, f32[8,64,256]{2,1,0:T(8,128)S(1)} %own_pairs.1.part_ref), custom_call_target="tpu_custom_call" | custom-call | tf_op jit(solution)/shard_map/halo_x/pallas_call | solution.py:241
  24.2 0.0 collective-permute-done.2.low_ref
  24.3 0.0 collective-permute-done.3.high_ref
  24.3 11.6 %halo_y.1 = (f32[8,64,256]{2,1,0:T(8,128)S(1)}, f32[8,64,64]{2,1,0:T(8,128)S(1)}, f32[8,64,64]{2,1,0:T(8,128)S(1)}, f32[64,64]{1,0:T(8,128)S(1)}, f32[64,64]{1,0:T(8,128)S(1)}, /*index=5*/f32[16,32,128]{2,1,0:T(8,128)S(1)}) custom-call(s32[5]{0:T(128)} %rank_ref.5, bf16[8,3,256]{2,1,0:T(4,128)(2,1)} %bitcast.13, ...), custom_call_target="tpu_custom_call" | custom-call | tf_op jit(solution)/shard_map/halo_y/pallas_call | solution.py:448
  35.8 16.5 %all_to_all.10.gram_in = f32[16,32,128]{2,1,0:T(8,128)S(1)} all-to-all(f32[16,32,128]{2,1,0:T(8,128)S(1)} %get-tuple-element.37), channel_id=1, replica_groups={{0,1,2,3,16,17,18,19,32,33,34,35,48,49,50,51},{4,5,6,7,20,21,22,23,36,3..., dimensions={0} | all-to-all | bytes 524288 | tf_op jit(solution)/shard_map/all_to_all | solution.py:558
  52.3 5.7 %upper23.1 = (f32[8,64,64]{2,1,0:T(8,128)}, bf16[8,64,256]{2,1,0:T(8,128)(2,1)}, f32[64,64]{1,0:T(8,128)S(1)}, f32[64,64]{1,0:T(8,128)S(1)}, f32[64,64]{1,0:T(8,...) custom-call(s32[5]{0:T(128)} %rank_ref.5, f32[16,32,128]{2,1,0:T(8,128)S(1)} %all_to_all.10.gram_in, ...), custom_call_target="tpu_custom_call" | custom-call | tf_op jit(solution)/shard_map/upper23/pallas_call | solution.py:504
  58.0 16.4 %all_to_all.11.gram_in = f32[4,32,128]{2,1,0:T(8,128)S(1)} all-to-all(f32[4,32,128]{2,1,0:T(8,128)S(1)} %get-tuple-element.45), channel_id=1, replica_groups={{0,4,64,68},{1,5,65,69},{2,6,66,70},{3,7,67,71},{8,12,72,76},{9,13,73,7..., dimensions={0} | all-to-all | bytes 131072 | tf_op jit(solution)/shard_map/all_to_all | solution.py:558
  74.4 2.9 %upper4.1 = (f32[3,64,64]{2,1,0:T(8,128)}, f32[64,64]{1,0:T(8,128)}) custom-call(s32[5]{0:T(128)} %rank_ref.5, f32[4,32,128]{2,1,0:T(8,128)S(1)} %all_to_all.11.gram_in, f32[64,64]{1,0:T(8,128)S(1)} %get-tuple-element.46.inv3_in, f32[64,64]{1,0:T(8,128)S(1)} %get-tuple-element.47.cur2_in, f32[64,64]{1,0:T(8,128)S(1)} %get-tuple-element.48.cur3_in, ...), custom_call_target="tpu_custom_call" | custom-call | tf_op jit(solution)/shard_map/upper4/pallas_call | solution.py:528
  (1 shorter events, 0.0 us)
Async XLA Ops:
  3.0 13.7 %collective-permute-start = (bf16[4,67,256]{2,1,0:T(8,128)(2,1)S(1)}, bf16[4,67,256]{2,1,0:T(8,128)(2,1)S(1)}, u32[]{:S(2)}, u32[]{:S(2)}) collective-permute-start(bf16[4,67,256]{2,1,0:T(8,128)(2,1)S(1)} %get-tuple-element.28), channel_id=1, source_target_pairs={{0,16},{16,32},{32,48},{48,64},{64,80},{80,96},{96,112},{112,128},... | collective-permute-start | bytes 411656 | tf_op jit(solution)/shard_map/ppermute | solution.py:540
  6.4 10.3 %collective-permute-start.1 = (bf16[4,67,256]{2,1,0:T(8,128)(2,1)S(1)}, bf16[4,67,256]{2,1,0:T(8,128)(2,1)S(1)}, u32[]{:S(2)}, u32[]{:S(2)}) collective-permute-start(bf16[4,67,256]{2,1,0:T(8,128)(2,1)S(1)} %get-tuple-element.29), channel_id=1, source_target_pairs={{16,0},{32,16},{48,32},{64,48},{80,64},{96,80},{112,96},{128,112},... | collective-permute-start | bytes 411656 | tf_op jit(solution)/shard_map/ppermute | solution.py:540
  16.8 7.5 %collective-permute-start.2 = (bf16[8,67,256]{2,1,0:T(8,128)(2,1)S(1)}, bf16[8,67,256]{2,1,0:T(8,128)(2,1)S(1)}, u32[]{:S(2)}, u32[]{:S(2)}) collective-permute-start(bf16[8,67,256]{2,1,0:T(8,128)(2,1)S(1)} %get-tuple-element.34), channel_id=1, source_target_pairs={{0,1},{1,2},{2,3},{3,4},{4,5},{5,6},{6,7},{7,8},{8,9},{9,10},{10,1... | collective-permute-start | bytes 823304 | tf_op jit(solution)/shard_map/ppermute | solution.py:540
  18.1 6.2 %collective-permute-start.3 = (bf16[8,67,256]{2,1,0:T(8,128)(2,1)S(1)}, bf16[8,67,256]{2,1,0:T(8,128)(2,1)S(1)}, u32[]{:S(2)}, u32[]{:S(2)}) collective-permute-start(bf16[8,67,256]{2,1,0:T(8,128)(2,1)S(1)} %get-tuple-element.35), channel_id=1, source_target_pairs={{1,0},{2,1},{3,2},{4,3},{5,4},{6,5},{7,6},{8,7},{9,8},{10,9},{11,1... | collective-permute-start | bytes 823304 | tf_op jit(solution)/shard_map/ppermute | solution.py:540
